TPU v7x, 128 devices: a whole 4x4x4 slice. The times are simulated.
128 devices in a mesh: row: 8 (over z, core), col: 16 (over y, x).
Axes of the slice: x: 4, y: 4, z: 4, core: 2. Of those that a mesh axis runs over, the one named last changes fastest.
Arguments:
- points: float32 [524288, 64], P(('row', 'col')), may hold values from -6 to 6
- factor: float32 [524288, 512], P(('row', 'col')), may hold values from -0.06 to 0.06
- pivots: int32 [2, 128], replicated, may hold values from 0 to 524287, as said below
Outputs:
- factor_new: float32 [524288, 256], P(('row', 'col'))
- gram_rows: float32 [256, 768], replicated
Inputs may be any that keep to these rules, and one draw needn't show every extreme that they name: All 256 pivots are different points.
All inputs are finite; a program needn't handle non-finite values.
Results may differ from a plain program's by a relative error of at most 0.00013.
Values sent between devices are 32-bit elements; how exact they have to be, the bound alone decides.
A program may use at most 128 MiB of HBM per device.

v0:
```python
import functools

import jax
import jax.numpy as jnp
from jax import lax
from jax.experimental import pallas as pl
from jax.experimental.pallas import tpu as pltpu
from jax.sharding import PartitionSpec as P

f32 = jnp.float32
bf16 = jnp.bfloat16
MESH = pl.DeviceIdType.MESH
CHIPS = 64
NUGGET = 0.1
MB = 1 << 20

NT = (((1,), (1,)), ((), ()))
TN = (((0,), (0,)), ((), ()))
NN = (((1,), (0,)), ((), ()))


def exact(a, b, dims=NN):
    return lax.dot_general(a, b, dims, precision=lax.Precision.HIGHEST, preferred_element_type=f32)


def mm(a, b, dims=NN):
    return lax.dot_general(a, b, dims, preferred_element_type=f32)


def halves(a):
    high = a.astype(bf16)
    return high, (a - high.astype(f32)).astype(bf16)


def offsets():
    def hops(d):
        return sum(min(c, 4 - c) for c in (d // 16, d // 4 % 4, d % 4))

    return sorted(range(1, CHIPS), key=lambda d: (-hops(d), d))


class Place:
    def __init__(self):
        row, col = lax.axis_index("row"), lax.axis_index("col")
        self.core, z = row % 2, row // 2
        y, x = col // 4, col % 4
        self.chip = z * 16 + col
        self.number = row * 16 + col
        self.other = (row + 1 - 2 * self.core, col)
        zs = [(z + i) % 4 for i in range(4)]
        ys = [(y + i) % 4 for i in range(4)]
        xs = [(x + i) % 4 for i in range(4)]
        self.peers = []
        for d in offsets():
            pz, pc = zs[d // 16], ys[d // 4 % 4] * 4 + xs[d % 4]
            self.peers.append(((pz * 2 + self.core, pc), pz * 16 + pc))


def greet(place):
    barrier = pltpu.get_barrier_semaphore()
    for device, _ in place.peers:
        pl.semaphore_signal(barrier, inc=1, device_id=device, device_id_type=MESH)
    pl.semaphore_signal(barrier, inc=1, device_id=place.other, device_id_type=MESH)


def greeted():
    pl.semaphore_wait(pltpu.get_barrier_semaphore(), CHIPS)


def remote(src, dst, send, recv, device):
    return pltpu.make_async_remote_copy(src, dst, send, recv, device_id=device, device_id_type=MESH)


def device_sum(place, mine, pair, arrived, own, total, send, recv):
    core, chip, other = place.core, place.chip, place.other
    swap = remote(mine.at[1 - core], pair, send.at[0], recv.at[0], other)
    swap.start()
    swap.wait_recv()
    pair[...] = mine[core] + pair[...]
    for slot, (device, target) in enumerate(place.peers):
        remote(pair.at[target], arrived.at[slot], send.at[1], recv.at[1], device).start()
    remote(arrived, arrived, send.at[1], recv.at[1], other).wait_recv()
    own[...] = pair[chip] + jnp.sum(arrived[...], axis=0)
    for device, _ in place.peers:
        remote(own, total.at[core, chip], send.at[2], recv.at[2], device).start()
    total[core, chip] = own[...]
    remote(arrived, arrived, send.at[2], recv.at[2], other).wait_recv()
    back = remote(total.at[core], total.at[core], send.at[3], recv.at[3], other)
    back.start()
    swap.wait_send()
    remote(arrived, arrived, send.at[1], recv.at[1], other).wait_send()
    remote(arrived, arrived, send.at[2], recv.at[2], other).wait_send()
    back.wait()


def sum_scratch(rows):
    return [
        pltpu.VMEM((2, CHIPS, rows, 128), f32),
        pltpu.VMEM((CHIPS, rows, 128), f32),
        pltpu.VMEM((CHIPS - 1, rows, 128), f32),
        pltpu.VMEM((rows, 128), f32),
        pltpu.VMEM((2, CHIPS, rows, 128), f32),
        pltpu.SemaphoreType.DMA((4,)),
        pltpu.SemaphoreType.DMA((4,)),
    ]


def fetch_kernel(pivots, points_hbm, factor_hbm, q_ref, p_ref, points, factor, load, mine, *rest):
    place = Place()
    greet(place)
    loads = [
        pltpu.make_async_copy(points_hbm, points, load.at[0]),
        pltpu.make_async_copy(factor_hbm, factor, load.at[1]),
    ]
    for copy in loads:
        copy.start()
    count, width = points.shape
    first = place.number * count
    for copy in loads:
        copy.wait()

    def pick(i, carry):
        rows = []
        for s in range(2):
            local = pivots[s, i] - first
            inside = ((local >= 0) & (local < count)).astype(jnp.int32).astype(f32)
            local = jnp.clip(local, 0, count - 1)
            rows.append((points[pl.ds(local, 1), :] * inside, factor[pl.ds(local, 1), :] * inside))
        half, chip = i // CHIPS, i % CHIPS
        for s in range(2):
            for j in range(4):
                mine[half, chip, pl.ds(4 * s + j, 1), :] = rows[s][1][:, 128 * j : 128 * (j + 1)]
        mine[half, chip, pl.ds(8, 1), :] = jnp.concatenate([rows[0][0], rows[1][0]], axis=1)
        return carry

    lax.fori_loop(0, 2 * CHIPS, pick, 0, unroll=4)
    greeted()
    total = rest[3]
    device_sum(place, mine, *rest)
    for half in range(2):
        for s in range(2):
            for j in range(4):
                q_ref[pl.ds(128 * s + CHIPS * half, CHIPS), pl.ds(128 * j, 128)] = total[half, :, 4 * s + j, :]
        p_ref[pl.ds(CHIPS * half, CHIPS), :] = total[half, :, 8, :]


def fetch(points, factor, pivots):
    return pl.pallas_call(
        fetch_kernel,
        out_shape=(jax.ShapeDtypeStruct((256, 512), f32), jax.ShapeDtypeStruct((128, 128), f32)),
        in_specs=[
            pl.BlockSpec(memory_space=pltpu.SMEM),
            pl.BlockSpec(memory_space=pl.ANY),
            pl.BlockSpec(memory_space=pl.ANY),
        ],
        out_specs=(pl.BlockSpec(memory_space=pltpu.VMEM), pl.BlockSpec(memory_space=pltpu.VMEM)),
        scratch_shapes=[
            pltpu.VMEM(points.shape, f32),
            pltpu.VMEM(factor.shape, f32),
            pltpu.SemaphoreType.DMA((2,)),
            *sum_scratch(9),
        ],
        compiler_params=pltpu.CompilerParams(collective_id=0, has_side_effects=True, vmem_limit_bytes=40 * MB),
    )(pivots, points, factor)


def residual_kernel(points, factor, q_ref, p_ref, r_ref, m_ref, qh, ql, pt, pn, cross):
    step = pl.program_id(0)
    width = points.shape[1]

    @pl.when(step == 0)
    def _():
        q = q_ref[...].T
        qh[...], ql[...] = halves(q)
        pp = p_ref[...].T
        p = jnp.concatenate([pp[:width], pp[width:]], axis=1) * (2.0 / width)
        high, low = halves(p)
        pt[...] = jnp.concatenate([high, low, high, low], axis=0)
        pn[...] = jnp.sum(p * p, axis=0, keepdims=True) * (width / 4.0)
        m_ref[...] = jnp.zeros_like(m_ref)
        cross[...] = jnp.zeros_like(cross)

    a = points[...]
    high, low = halves(a)
    inner = mm(jnp.concatenate([high, high, low, low], axis=1), pt[...])
    norm = jnp.sum(a * a, axis=1, keepdims=True) * (1.0 / width)
    kernel = jnp.exp(inner - norm - pn[...])
    xh, xl = halves(factor[...])
    r = kernel - (mm(xh, qh[...]) + mm(xh, ql[...]) + mm(xl, qh[...]))
    r_ref[...] = r
    rh, rl = halves(r)
    wide = factor.shape[1]
    m_ref[:, :wide] += mm(rh, xh, TN) + mm(rh, xl, TN) + mm(rl, xh, TN)
    m_ref[:, wide:] += mm(rh, rh, TN)
    cross[...] += mm(rh, rl, TN)

    @pl.when(step == pl.num_programs(0) - 1)
    def _():
        m_ref[:, wide:] += cross[...] + cross[...].T


def residual(points, factor, q, p, tile=256):
    count, width = points.shape
    wide = factor.shape[1]
    size = q.shape[0]
    return pl.pallas_call(
        residual_kernel,
        out_shape=(jax.ShapeDtypeStruct((count, size), f32), jax.ShapeDtypeStruct((size, wide + size), f32)),
        grid=(count // tile,),
        in_specs=[
            pl.BlockSpec((tile, width), lambda i: (i, 0)),
            pl.BlockSpec((tile, wide), lambda i: (i, 0)),
            pl.BlockSpec(q.shape, lambda i: (0, 0)),
            pl.BlockSpec(p.shape, lambda i: (0, 0)),
        ],
        out_specs=(
            pl.BlockSpec((tile, size), lambda i: (i, 0)),
            pl.BlockSpec((size, wide + size), lambda i: (0, 0)),
        ),
        scratch_shapes=[
            pltpu.VMEM((wide, size), bf16),
            pltpu.VMEM((wide, size), bf16),
            pltpu.VMEM((4 * width, size), bf16),
            pltpu.VMEM((1, size), f32),
            pltpu.VMEM((size, size), f32),
        ],
        compiler_params=pltpu.CompilerParams(vmem_limit_bytes=40 * MB),
    )(points, factor, q, p)


def inverse_lower(core, a_ref, t_ref):
    size = core.shape[0]
    rows = lax.broadcasted_iota(jnp.int32, (size, size), 0)
    cols = lax.broadcasted_iota(jnp.int32, (size, size), 1)
    a_ref[...] = core
    t_ref[...] = (rows == cols).astype(f32)
    row = lax.broadcasted_iota(jnp.int32, (size, 1), 0)

    def step(b, carry):
        first = b * 8
        for i in range(8):
            at = first + i
            line = a_ref[pl.ds(at, 1), :]
            made = t_ref[pl.ds(at, 1), :]
            pivot = line[:, i : i + 1]
            scale = jnp.where(row > at, a_ref[:, i : i + 1] * (1.0 / pivot), 0.0)
            scale = jnp.where(row == at, 1.0 - lax.rsqrt(pivot), scale)
            a_ref[...] = a_ref[...] - scale * line
            t_ref[...] = t_ref[...] - scale * made
        a_ref[...] = pltpu.roll(a_ref[...], size - 8, 1)
        return carry

    lax.fori_loop(0, size // 8, step, 0)
    return t_ref[...]


def weights_kernel(q_ref, p_ref, w_ref, a_ref, t_ref):
    q = q_ref[...]
    pp = p_ref[...]
    size, width = pp.shape[0], pp.shape[1] // 2
    p = jnp.concatenate([pp[:, :width], pp[:, width:]], axis=0)
    norm = jnp.sum(p * p, axis=1, keepdims=True)
    across = exact(jnp.ones((8, width), f32), p * p, NT)[:1]
    kernel = jnp.exp((2.0 * exact(p, p, NT) - norm - across) * (1.0 / width))
    outer = exact(q, q, NT)
    rows = lax.broadcasted_iota(jnp.int32, (size, size), 0)
    cols = lax.broadcasted_iota(jnp.int32, (size, size), 1)
    eye = (rows == cols).astype(f32)

    def core(k, g):
        shift = NUGGET + jnp.max(jnp.sum(jnp.abs(g), axis=1, keepdims=True), axis=0, keepdims=True)
        return k - g + shift * eye

    t0 = inverse_lower(core(kernel[:size, :size], outer[:size, :size]), a_ref, t_ref)
    c10 = exact(kernel[size:, :size] - outer[size:, :size], t0, NT)
    g1 = outer[size:, size:] + exact(c10, c10, NT)
    t1 = inverse_lower(core(kernel[size:, size:], g1), a_ref, t_ref)
    t10 = -exact(exact(t1, c10), t0)
    w_ref[:size, :size] = t0.T
    w_ref[:size, size:] = t10.T
    w_ref[size:, :size] = jnp.zeros((size, size), f32)
    w_ref[size:, size:] = t1.T


def weights(q, p):
    size = q.shape[0]
    return pl.pallas_call(
        weights_kernel,
        out_shape=jax.ShapeDtypeStruct((size, size), f32),
        in_specs=[pl.BlockSpec(memory_space=pltpu.VMEM)] * 2,
        out_specs=pl.BlockSpec(memory_space=pltpu.VMEM),
        scratch_shapes=[pltpu.VMEM((size // 2, size // 2), f32)] * 2,
        compiler_params=pltpu.CompilerParams(vmem_limit_bytes=40 * MB),
    )(q, p)


def total_kernel(m_ref, o_ref, mine, *rest):
    place = Place()
    greet(place)
    for k in range(2):
        for h in range(2):
            for j in range(6):
                mine[k, :, 2 * j + h, :] = m_ref[pl.ds(128 * k + CHIPS * h, CHIPS), pl.ds(128 * j, 128)]
    greeted()
    total = rest[3]
    device_sum(place, mine, *rest)
    for k in range(2):
        for h in range(2):
            for j in range(6):
                o_ref[pl.ds(128 * k + CHIPS * h, CHIPS), pl.ds(128 * j, 128)] = total[k, :, 2 * j + h, :]


def total_products(m):
    return pl.pallas_call(
        total_kernel,
        out_shape=jax.ShapeDtypeStruct(m.shape, f32),
        in_specs=[pl.BlockSpec(memory_space=pltpu.VMEM)],
        out_specs=pl.BlockSpec(memory_space=pltpu.VMEM),
        scratch_shapes=sum_scratch(12),
        compiler_params=pltpu.CompilerParams(collective_id=1, has_side_effects=True, vmem_limit_bytes=40 * MB),
    )(m)


def columns_kernel(r_ref, w_ref, m_ref, c_ref, g_ref, wh, wl, *, scale):
    @pl.when(pl.program_id(0) == 0)
    def _():
        w = w_ref[...]
        wh[...], wl[...] = halves(w)
        size = w.shape[0]
        wide = m_ref.shape[1] - size
        turned = w.T
        g_ref[:, :wide] = exact(turned, m_ref[:, :wide]) * scale
        g_ref[:, wide:] = exact(turned, exact(m_ref[:, wide:], w)) * scale

    rh, rl = halves(r_ref[...])
    c_ref[...] = mm(rh, wh[...]) + mm(rh, wl[...]) + mm(rl, wh[...])


def columns(r, w, m, tile=512):
    count, size = r.shape
    return pl.pallas_call(
        functools.partial(columns_kernel, scale=1.0 / count),
        out_shape=(jax.ShapeDtypeStruct(r.shape, f32), jax.ShapeDtypeStruct(m.shape, f32)),
        grid=(count // tile,),
        in_specs=[
            pl.BlockSpec((tile, size), lambda i: (i, 0)),
            pl.BlockSpec(w.shape, lambda i: (0, 0)),
            pl.BlockSpec(m.shape, lambda i: (0, 0)),
        ],
        out_specs=(pl.BlockSpec((tile, size), lambda i: (i, 0)), pl.BlockSpec(m.shape, lambda i: (0, 0))),
        scratch_shapes=[pltpu.VMEM(w.shape, bf16)] * 2,
        compiler_params=pltpu.CompilerParams(vmem_limit_bytes=40 * MB),
    )(r, w, m)


def body(points, factor, pivots):
    q, p = fetch(points, factor, pivots)
    r, m = residual(points, factor, q, p)
    w = weights(q, p)
    m = total_products(m)
    return columns(r, w, m)


def solution(mesh):
    split = P(("row", "col"), None)
    return jax.shard_map(
        body,
        mesh=mesh,
        in_specs=(split, split, P()),
        out_specs=(split, P()),
        check_vma=False,
    )
```

profile of v0, /device:TPU:1, one launch (start us, length us, event | category | flops | bytes accessed | tf_op | source)
XLA Modules:
  0.0 116.7 jit_solution(3977906234798520346)
XLA Ops:
  0.6 1.8 %copy.6.points_hbm.points = f32[4096,64]{1,0:T(8,128)S(1)} copy(f32[4096,64]{0,1:T(8,128)} %param.3) | data formatting | bytes 2097152 | tf_op args[0]
  2.5 0.0 copy-start
  2.5 3.4 %copy-done = f32[4096,512]{1,0:T(8,128)S(1)} copy-done((f32[4096,512]{1,0:T(8,128)S(1)}, f32[4096,512]{1,0:T(8,128)}, u32[]{:S(2)}) %copy-start) | copy-done | bytes 8388632
  5.8 0.0 copy-start.1
  5.8 0.7 copy-done.1
  6.5 27.8 %shard_map.50 = (f32[256,512]{1,0:T(8,128)S(1)}, f32[128,128]{1,0:T(8,128)S(1)}) custom-call(s32[2,128]{1,0:T(2,128)S(1)} %copy-done.1, f32[4096,64]{1,0:T(8,128)S(1)} %copy.6.points_hbm.points, f32[4096,512]{1,0:T(8,128)S(1)} %copy-done), custom_call_target="tpu_custom_call" | custom-call | tf_op jit(solution)/shard_map/pallas_call | solution.py:148
  34.4 29.4 %shard_map.52.w_ref = f32[256,256]{1,0:T(8,128)S(1)} custom-call(f32[256,512]{1,0:T(8,128)S(1)} %get-tuple-element.6.q_ref, f32[128,128]{1,0:T(8,128)S(1)} %get-tuple-element.7.p_ref), custom_call_target="tpu_custom_call" | custom-call | tf_op jit(solution)/shard_map/pallas_call | solution.py:287
  63.8 22.3 %shard_map.51 = (f32[4096,256]{1,0:T(8,128)S(1)}, f32[256,768]{1,0:T(8,128)S(1)}) custom-call(f32[4096,64]{1,0:T(8,128)S(1)} %copy.6.points_hbm.points, f32[4096,512]{1,0:T(8,128)} %factor.1, f32[256,512]{1,0:T(8,128)S(1)} %get-tuple-element.6.q_ref, f32[128,128]{1,0:T(8,128)S(1)} %get-tuple-element.7.p_ref), custom_call_target="tpu_custom_call" | custom-call | tf_op jit(solution)/shard_map/pallas_call | solution.py:206
  86.1 23.8 %shard_map.53.m_ref = f32[256,768]{1,0:T(8,128)S(1)} custom-call(f32[256,768]{1,0:T(8,128)S(1)} %get-tuple-element.9.m_ref), custom_call_target="tpu_custom_call" | custom-call | tf_op jit(solution)/shard_map/pallas_call | solution.py:314
  110.0 6.8 %shard_map.54 = (f32[4096,256]{1,0:T(8,128)}, f32[256,768]{1,0:T(8,128)}) custom-call(f32[4096,256]{1,0:T(8,128)S(1)} %get-tuple-element.8.r_ref, f32[256,256]{1,0:T(8,128)S(1)} %shard_map.52.w_ref, f32[256,768]{1,0:T(8,128)S(1)} %shard_map.53.m_ref), custom_call_target="tpu_custom_call" | custom-call | tf_op jit(solution)/shard_map/pallas_call | solution.py:341
Async XLA Ops:
  2.5 3.4 %copy-start = (f32[4096,512]{1,0:T(8,128)S(1)}, f32[4096,512]{1,0:T(8,128)}, u32[]{:S(2)}) copy-start(f32[4096,512]{1,0:T(8,128)} %factor.1) | copy-start | bytes 25165828
  5.8 0.7 copy-start.1
where the time goes:
time: 117 us
  Pallas kernels  110 us (94%)
  local copies, waits for them, and re-layouts  5.88 us (5%)
    pallas_call x1, Pallas kernels, weights(): pl.pallas_call(weights_kernel, out_shape=jax.ShapeDtypeStruct((size, size...  29.4 us
    pallas_call x1, Pallas kernels, fetch(): pl.pallas_call(fetch_kernel, out_shape=(jax.ShapeDtypeStruct((256, 512),...  27.8 us
    pallas_call x1, Pallas kernels, total_products(): pl.pallas_call(total_kernel, out_shape=jax.ShapeDtypeStruct(m.shape, f32)...  23.8 us
    pallas_call x1, Pallas kernels, residual(): pl.pallas_call(residual_kernel, out_shape=(jax.ShapeDtypeStruct((count, s...  22.3 us
    pallas_call x1, Pallas kernels, columns(): pl.pallas_call(functools.partial(columns_kernel, scale=1.0 / count), out_...  6.76 us
    unnamed x5, local copies, waits for them, and re-layouts  5.88 us

commit v1 on v0

--- a/solution.py
+++ b/solution.py
@@ -71,7 +71,7 @@
     return pltpu.make_async_remote_copy(src, dst, send, recv, device_id=device, device_id_type=MESH)
 
 
-def device_sum(place, mine, pair, arrived, own, total, send, recv):
+def device_sum(place, mine, pair, arrived, own, total, send, recv, first=None, second=None):
     core, chip, other = place.core, place.chip, place.other
     swap = remote(mine.at[1 - core], pair, send.at[0], recv.at[0], other)
     swap.start()
@@ -79,11 +79,15 @@
     pair[...] = mine[core] + pair[...]
     for slot, (device, target) in enumerate(place.peers):
         remote(pair.at[target], arrived.at[slot], send.at[1], recv.at[1], device).start()
+    if first is not None:
+        first()
     remote(arrived, arrived, send.at[1], recv.at[1], other).wait_recv()
     own[...] = pair[chip] + jnp.sum(arrived[...], axis=0)
     for device, _ in place.peers:
         remote(own, total.at[core, chip], send.at[2], recv.at[2], device).start()
     total[core, chip] = own[...]
+    if second is not None:
+        second()
     remote(arrived, arrived, send.at[2], recv.at[2], other).wait_recv()
     back = remote(total.at[core], total.at[core], send.at[3], recv.at[3], other)
     back.start()
@@ -254,47 +258,25 @@
     return t_ref[...]
 
 
-def weights_kernel(q_ref, p_ref, w_ref, a_ref, t_ref):
+def pivot_terms(q_ref, p_ref, core_ref):
     q = q_ref[...]
     pp = p_ref[...]
-    size, width = pp.shape[0], pp.shape[1] // 2
+    width = pp.shape[1] // 2
     p = jnp.concatenate([pp[:, :width], pp[:, width:]], axis=0)
     norm = jnp.sum(p * p, axis=1, keepdims=True)
     across = exact(jnp.ones((8, width), f32), p * p, NT)[:1]
-    kernel = jnp.exp((2.0 * exact(p, p, NT) - norm - across) * (1.0 / width))
-    outer = exact(q, q, NT)
-    rows = lax.broadcasted_iota(jnp.int32, (size, size), 0)
-    cols = lax.broadcasted_iota(jnp.int32, (size, size), 1)
-    eye = (rows == cols).astype(f32)
-
-    def core(k, g):
-        shift = NUGGET + jnp.max(jnp.sum(jnp.abs(g), axis=1, keepdims=True), axis=0, keepdims=True)
-        return k - g + shift * eye
-
-    t0 = inverse_lower(core(kernel[:size, :size], outer[:size, :size]), a_ref, t_ref)
-    c10 = exact(kernel[size:, :size] - outer[size:, :size], t0, NT)
-    g1 = outer[size:, size:] + exact(c10, c10, NT)
-    t1 = inverse_lower(core(kernel[size:, size:], g1), a_ref, t_ref)
-    t10 = -exact(exact(t1, c10), t0)
-    w_ref[:size, :size] = t0.T
-    w_ref[:size, size:] = t10.T
-    w_ref[size:, :size] = jnp.zeros((size, size), f32)
-    w_ref[size:, size:] = t1.T
-
-
-def weights(q, p):
-    size = q.shape[0]
-    return pl.pallas_call(
-        weights_kernel,
-        out_shape=jax.ShapeDtypeStruct((size, size), f32),
-        in_specs=[pl.BlockSpec(memory_space=pltpu.VMEM)] * 2,
-        out_specs=pl.BlockSpec(memory_space=pltpu.VMEM),
-        scratch_shapes=[pltpu.VMEM((size // 2, size // 2), f32)] * 2,
-        compiler_params=pltpu.CompilerParams(vmem_limit_bytes=40 * MB),
-    )(q, p)
-
-
-def total_kernel(m_ref, o_ref, mine, *rest):
+    core_ref[0] = jnp.exp((2.0 * exact(p, p, NT) - norm - across) * (1.0 / width))
+    core_ref[1] = exact(q, q, NT)
+
+
+def shifted(k, g):
+    rows = lax.broadcasted_iota(jnp.int32, g.shape, 0)
+    cols = lax.broadcasted_iota(jnp.int32, g.shape, 1)
+    shift = NUGGET + jnp.max(jnp.sum(jnp.abs(g), axis=1, keepdims=True), axis=0, keepdims=True)
+    return k - g + shift * (rows == cols).astype(f32)
+
+
+def total_kernel(m_ref, q_ref, p_ref, o_ref, w_ref, core_ref, a_ref, t_ref, mine, *rest):
     place = Place()
     greet(place)
     for k in range(2):
@@ -303,22 +285,45 @@
                 mine[k, :, 2 * j + h, :] = m_ref[pl.ds(128 * k + CHIPS * h, CHIPS), pl.ds(128 * j, 128)]
     greeted()
     total = rest[3]
-    device_sum(place, mine, *rest)
+    size = a_ref.shape[0]
+
+    def first():
+        pivot_terms(q_ref, p_ref, core_ref)
+        t0 = inverse_lower(shifted(core_ref[0, :size, :size], core_ref[1, :size, :size]), a_ref, t_ref)
+        w_ref[:size, :size] = t0.T
+        w_ref[size:, :size] = jnp.zeros((size, size), f32)
+
+    def second():
+        turned = w_ref[:size, :size]
+        c10 = exact(core_ref[0, size:, :size] - core_ref[1, size:, :size], turned)
+        g1 = core_ref[1, size:, size:] + exact(c10, c10, NT)
+        t1 = inverse_lower(shifted(core_ref[0, size:, size:], g1), a_ref, t_ref)
+        w_ref[size:, size:] = t1.T
+        w_ref[:size, size:] = -exact(turned, exact(t1, c10), NT)
+
+    device_sum(place, mine, *rest, first, second)
     for k in range(2):
         for h in range(2):
             for j in range(6):
                 o_ref[pl.ds(128 * k + CHIPS * h, CHIPS), pl.ds(128 * j, 128)] = total[k, :, 2 * j + h, :]
 
 
-def total_products(m):
+def total_products(m, q, p):
+    size = q.shape[0]
+    half = size // 2
     return pl.pallas_call(
         total_kernel,
-        out_shape=jax.ShapeDtypeStruct(m.shape, f32),
-        in_specs=[pl.BlockSpec(memory_space=pltpu.VMEM)],
-        out_specs=pl.BlockSpec(memory_space=pltpu.VMEM),
-        scratch_shapes=sum_scratch(12),
+        out_shape=(jax.ShapeDtypeStruct(m.shape, f32), jax.ShapeDtypeStruct((size, size), f32)),
+        in_specs=[pl.BlockSpec(memory_space=pltpu.VMEM)] * 3,
+        out_specs=(pl.BlockSpec(memory_space=pltpu.VMEM),) * 2,
+        scratch_shapes=[
+            pltpu.VMEM((2, size, size), f32),
+            pltpu.VMEM((half, half), f32),
+            pltpu.VMEM((half, half), f32),
+            *sum_scratch(12),
+        ],
         compiler_params=pltpu.CompilerParams(collective_id=1, has_side_effects=True, vmem_limit_bytes=40 * MB),
-    )(m)
+    )(m, q, p)
 
 
 def columns_kernel(r_ref, w_ref, m_ref, c_ref, g_ref, wh, wl, *, scale):
@@ -356,8 +361,7 @@
 def body(points, factor, pivots):
     q, p = fetch(points, factor, pivots)
     r, m = residual(points, factor, q, p)
-    w = weights(q, p)
-    m = total_products(m)
+    m, w = total_products(m, q, p)
     return columns(r, w, m)
 
 

time: 117 us -> 102 us (0.87)
  Pallas kernels: 110 us -> 95.2 us
    pallas_call x2 -> x1, Pallas kernels: 53.3 us -> 38.3 us  [total_products(): pl.pallas_call(total_kernel, out_shape=(jax.ShapeDtypeStruct(m.shape, f32...]
where the time goes in v1:
time: 102 us
  Pallas kernels  95.2 us (93%)
  local copies, waits for them, and re-layouts  5.88 us (6%)
    pallas_call x1, Pallas kernels, total_products(): pl.pallas_call(total_kernel, out_shape=(jax.ShapeDtypeStruct(m.shape, f32...  38.3 us
    pallas_call x1, Pallas kernels, fetch(): pl.pallas_call(fetch_kernel, out_shape=(jax.ShapeDtypeStruct((256, 512),...  27.8 us
    pallas_call x1, Pallas kernels, residual(): pl.pallas_call(residual_kernel, out_shape=(jax.ShapeDtypeStruct((count, s...  22.3 us
    pallas_call x1, Pallas kernels, columns(): pl.pallas_call(functools.partial(columns_kernel, scale=1.0 / count), out_...  6.76 us
    unnamed x5, local copies, waits for them, and re-layouts  5.88 us

profile of v1, /device:TPU:1, one launch (start us, length us, event | category | flops | bytes accessed | tf_op | source)
XLA Modules:
  0.0 101.7 jit_solution(12324036267059078902)
XLA Ops:
  0.6 1.8 %copy.6.points_hbm.points = f32[4096,64]{1,0:T(8,128)S(1)} copy(f32[4096,64]{0,1:T(8,128)} %param.3) | data formatting | bytes 2097152 | tf_op args[0]
  2.5 0.0 copy-start
  2.5 3.4 %copy-done = f32[4096,512]{1,0:T(8,128)S(1)} copy-done((f32[4096,512]{1,0:T(8,128)S(1)}, f32[4096,512]{1,0:T(8,128)}, u32[]{:S(2)}) %copy-start) | copy-done | bytes 8388632
  5.8 0.0 copy-start.1
  5.8 0.7 copy-done.1
  6.5 27.8 %shard_map.50 = (f32[256,512]{1,0:T(8,128)S(1)}, f32[128,128]{1,0:T(8,128)S(1)}) custom-call(s32[2,128]{1,0:T(2,128)S(1)} %copy-done.1, f32[4096,64]{1,0:T(8,128)S(1)} %copy.6.points_hbm.points, f32[4096,512]{1,0:T(8,128)S(1)} %copy-done), custom_call_target="tpu_custom_call" | custom-call | tf_op jit(solution)/shard_map/pallas_call | solution.py:152
  34.4 22.3 %shard_map.51 = (f32[4096,256]{1,0:T(8,128)S(1)}, f32[256,768]{1,0:T(8,128)S(1)}) custom-call(f32[4096,64]{1,0:T(8,128)S(1)} %copy.6.points_hbm.points, f32[4096,512]{1,0:T(8,128)} %factor.1, f32[256,512]{1,0:T(8,128)S(1)} %get-tuple-element.8.q_ref, f32[128,128]{1,0:T(8,128)S(1)} %get-tuple-element.9.p_ref), custom_call_target="tpu_custom_call" | custom-call | tf_op jit(solution)/shard_map/pallas_call | solution.py:210
  56.7 38.3 %shard_map.52 = (f32[256,768]{1,0:T(8,128)S(1)}, f32[256,256]{1,0:T(8,128)S(1)}) custom-call(f32[256,768]{1,0:T(8,128)S(1)} %get-tuple-element.11.m_ref, f32[256,512]{1,0:T(8,128)S(1)} %get-tuple-element.8.q_ref, f32[128,128]{1,0:T(8,128)S(1)} %get-tuple-element.9.p_ref), custom_call_target="tpu_custom_call" | custom-call | tf_op jit(solution)/shard_map/pallas_call | solution.py:314
  95.0 6.8 %shard_map.53 = (f32[4096,256]{1,0:T(8,128)}, f32[256,768]{1,0:T(8,128)}) custom-call(f32[4096,256]{1,0:T(8,128)S(1)} %get-tuple-element.10.r_ref, f32[256,256]{1,0:T(8,128)S(1)} %get-tuple-element.12.w_ref, f32[256,768]{1,0:T(8,128)S(1)} %get-tuple-element.13.m_ref), custom_call_target="tpu_custom_call" | custom-call | tf_op jit(solution)/shard_map/pallas_call | solution.py:346
Async XLA Ops:
  2.5 3.4 %copy-start = (f32[4096,512]{1,0:T(8,128)S(1)}, f32[4096,512]{1,0:T(8,128)}, u32[]{:S(2)}) copy-start(f32[4096,512]{1,0:T(8,128)} %factor.1) | copy-start | bytes 25165828
  5.8 0.7 copy-start.1

commit v2 on v1

--- a/solution.py
+++ b/solution.py
@@ -71,26 +71,27 @@
     return pltpu.make_async_remote_copy(src, dst, send, recv, device_id=device, device_id_type=MESH)
 
 
-def device_sum(place, mine, pair, arrived, own, total, send, recv, first=None, second=None):
+def device_sum(place, mine, pair, arrived, own, total, send, recv, work=None):
     core, chip, other = place.core, place.chip, place.other
     swap = remote(mine.at[1 - core], pair, send.at[0], recv.at[0], other)
+    work = work or [lambda: None] * 4
     swap.start()
+    work[0]()
     swap.wait_recv()
     pair[...] = mine[core] + pair[...]
     for slot, (device, target) in enumerate(place.peers):
         remote(pair.at[target], arrived.at[slot], send.at[1], recv.at[1], device).start()
-    if first is not None:
-        first()
+    work[1]()
     remote(arrived, arrived, send.at[1], recv.at[1], other).wait_recv()
     own[...] = pair[chip] + jnp.sum(arrived[...], axis=0)
     for device, _ in place.peers:
         remote(own, total.at[core, chip], send.at[2], recv.at[2], device).start()
     total[core, chip] = own[...]
-    if second is not None:
-        second()
+    work[2]()
     remote(arrived, arrived, send.at[2], recv.at[2], other).wait_recv()
     back = remote(total.at[core], total.at[core], send.at[3], recv.at[3], other)
     back.start()
+    work[3]()
     swap.wait_send()
     remote(arrived, arrived, send.at[1], recv.at[1], other).wait_send()
     remote(arrived, arrived, send.at[2], recv.at[2], other).wait_send()
@@ -109,19 +110,28 @@
     ]
 
 
-def fetch_kernel(pivots, points_hbm, factor_hbm, q_ref, p_ref, points, factor, load, mine, *rest):
+def fetch_kernel(pivots_hbm, points_hbm, factor_hbm, q_ref, p_ref, pivots, turned, points, factor, load, mine, *rest):
     place = Place()
-    greet(place)
     loads = [
-        pltpu.make_async_copy(points_hbm, points, load.at[0]),
-        pltpu.make_async_copy(factor_hbm, factor, load.at[1]),
+        pltpu.make_async_copy(points_hbm, turned, load.at[0]),
+        pltpu.make_async_copy(pivots_hbm, pivots, load.at[1]),
+        pltpu.make_async_copy(factor_hbm, factor, load.at[2]),
     ]
     for copy in loads:
         copy.start()
-    count, width = points.shape
+    greet(place)
+    count = points.shape[0]
     first = place.number * count
-    for copy in loads:
-        copy.wait()
+    loads[0].wait()
+
+    def turn(i, carry):
+        at = pl.multiple_of(i * 128, 128)
+        points[pl.ds(at, 128), :] = turned[:, pl.ds(at, 128)].T
+        return carry
+
+    lax.fori_loop(0, count // 128, turn, 0)
+    loads[1].wait()
+    loads[2].wait()
 
     def pick(i, carry):
         rows = []
@@ -149,62 +159,71 @@
 
 
 def fetch(points, factor, pivots):
+    width, count = points.shape
     return pl.pallas_call(
         fetch_kernel,
         out_shape=(jax.ShapeDtypeStruct((256, 512), f32), jax.ShapeDtypeStruct((128, 128), f32)),
-        in_specs=[
-            pl.BlockSpec(memory_space=pltpu.SMEM),
-            pl.BlockSpec(memory_space=pl.ANY),
-            pl.BlockSpec(memory_space=pl.ANY),
-        ],
+        in_specs=[pl.BlockSpec(memory_space=pltpu.HBM)] * 3,
         out_specs=(pl.BlockSpec(memory_space=pltpu.VMEM), pl.BlockSpec(memory_space=pltpu.VMEM)),
         scratch_shapes=[
-            pltpu.VMEM(points.shape, f32),
+            pltpu.SMEM(pivots.shape, jnp.int32),
+            pltpu.VMEM((width, count), f32),
+            pltpu.VMEM((count, width), f32),
             pltpu.VMEM(factor.shape, f32),
-            pltpu.SemaphoreType.DMA((2,)),
+            pltpu.SemaphoreType.DMA((3,)),
             *sum_scratch(9),
         ],
-        compiler_params=pltpu.CompilerParams(collective_id=0, has_side_effects=True, vmem_limit_bytes=40 * MB),
+        compiler_params=pltpu.CompilerParams(collective_id=0, has_side_effects=True, vmem_limit_bytes=51 * MB),
     )(pivots, points, factor)
 
 
-def residual_kernel(points, factor, q_ref, p_ref, r_ref, m_ref, qh, ql, pt, pn, cross):
+def residual_kernel(points, factor, q_ref, p_ref, r_ref, m_ref, qh, ql, pt, pn, cross, xa, ra, xb, rb):
     step = pl.program_id(0)
-    width = points.shape[1]
+    width = points.shape[0]
+    tile, wide = factor.shape[0] // 2, factor.shape[1]
 
     @pl.when(step == 0)
     def _():
-        q = q_ref[...].T
-        qh[...], ql[...] = halves(q)
+        qh[...], ql[...] = halves(q_ref[...].T)
         pp = p_ref[...].T
         p = jnp.concatenate([pp[:width], pp[width:]], axis=1) * (2.0 / width)
         high, low = halves(p)
         pt[...] = jnp.concatenate([high, low, high, low], axis=0)
         pn[...] = jnp.sum(p * p, axis=0, keepdims=True) * (width / 4.0)
-        m_ref[...] = jnp.zeros_like(m_ref)
-        cross[...] = jnp.zeros_like(cross)
-
-    a = points[...]
-    high, low = halves(a)
-    inner = mm(jnp.concatenate([high, high, low, low], axis=1), pt[...])
-    norm = jnp.sum(a * a, axis=1, keepdims=True) * (1.0 / width)
-    kernel = jnp.exp(inner - norm - pn[...])
-    xh, xl = halves(factor[...])
-    r = kernel - (mm(xh, qh[...]) + mm(xh, ql[...]) + mm(xl, qh[...]))
-    r_ref[...] = r
-    rh, rl = halves(r)
-    wide = factor.shape[1]
-    m_ref[:, :wide] += mm(rh, xh, TN) + mm(rh, xl, TN) + mm(rl, xh, TN)
-    m_ref[:, wide:] += mm(rh, rh, TN)
-    cross[...] += mm(rh, rl, TN)
+        for ref in (m_ref, cross, xb, rb):
+            ref[...] = jnp.zeros_like(ref)
+
+    def make(first, x, r):
+        a = points[:, first : first + tile]
+        high, low = halves(a)
+        inner = mm(jnp.concatenate([high, high, low, low], axis=0), pt[...], TN)
+        norm = jnp.sum(a * a, axis=0, keepdims=True) * (1.0 / width)
+        norm = jnp.broadcast_to(norm, (8, tile)).T[:, :1]
+        xh, xl = halves(factor[first : first + tile, :])
+        value = jnp.exp(inner - norm - pn[...]) - (mm(xh, qh[...]) + mm(xh, ql[...]) + mm(xl, qh[...]))
+        r_ref[first : first + tile, :] = value
+        x[0], x[1] = xh, xl
+        r[0], r[1] = halves(value)
+
+    def add(x, r):
+        rh, rl = r[0], r[1]
+        m_ref[:, :wide] += mm(rh, x[0], TN) + mm(rh, x[1], TN) + mm(rl, x[0], TN)
+        m_ref[:, wide:] += mm(rh, rh, TN)
+        cross[...] += mm(rh, rl, TN)
+
+    add(xb, rb)
+    make(0, xa, ra)
+    add(xa, ra)
+    make(tile, xb, rb)
 
     @pl.when(step == pl.num_programs(0) - 1)
     def _():
+        add(xb, rb)
         m_ref[:, wide:] += cross[...] + cross[...].T
 
 
-def residual(points, factor, q, p, tile=256):
-    count, width = points.shape
+def residual(points, factor, q, p, tile=512):
+    width, count = points.shape
     wide = factor.shape[1]
     size = q.shape[0]
     return pl.pallas_call(
@@ -212,7 +231,7 @@
         out_shape=(jax.ShapeDtypeStruct((count, size), f32), jax.ShapeDtypeStruct((size, wide + size), f32)),
         grid=(count // tile,),
         in_specs=[
-            pl.BlockSpec((tile, width), lambda i: (i, 0)),
+            pl.BlockSpec((width, tile), lambda i: (0, i)),
             pl.BlockSpec((tile, wide), lambda i: (i, 0)),
             pl.BlockSpec(q.shape, lambda i: (0, 0)),
             pl.BlockSpec(p.shape, lambda i: (0, 0)),
@@ -227,9 +246,45 @@
             pltpu.VMEM((4 * width, size), bf16),
             pltpu.VMEM((1, size), f32),
             pltpu.VMEM((size, size), f32),
+            *[pltpu.VMEM((2, tile // 2, wide), bf16), pltpu.VMEM((2, tile // 2, size), bf16)] * 2,
         ],
         compiler_params=pltpu.CompilerParams(vmem_limit_bytes=40 * MB),
     )(points, factor, q, p)
+
+
+def spread(a, rows):
+    return jnp.broadcast_to(a, (rows, 128))
+
+
+def panel_factor(block):
+    columns = [spread(block[:, i : i + 1], 8) for i in range(8)]
+    left = {(i, j): spread(columns[j][i : i + 1, :], 8) for i in range(8) for j in range(i, 8)}
+    lower, inverse = {}, {}
+    for i in range(8):
+        scale = lax.rsqrt(left[i, i])
+        for j in range(i + 1, 8):
+            lower[j, i] = left[i, j] * scale
+        for j in range(i + 1, 8):
+            for k in range(j, 8):
+                left[j, k] = left[j, k] - lower[j, i] * lower[k, i]
+        inverse[i, i] = scale
+        for j in range(i):
+            terms = [lower[i, k] * inverse[k, j] for k in range(j, i)]
+            inverse[i, j] = -functools.reduce(jnp.add, terms) * scale
+    row = lax.broadcasted_iota(jnp.int32, (8, 128), 0)
+    made = []
+    for j in range(8):
+        column = jnp.zeros((8, 128), f32)
+        for i in range(j, 8):
+            column = jnp.where(row == i, inverse[i, j], column)
+        made.append(column)
+    return made
+
+
+def thirds(a):
+    high = a.astype(bf16).astype(f32)
+    middle = (a - high).astype(bf16).astype(f32)
+    return high, middle, a - high - middle
 
 
 def inverse_lower(core, a_ref, t_ref):
@@ -238,20 +293,20 @@
     cols = lax.broadcasted_iota(jnp.int32, (size, size), 1)
     a_ref[...] = core
     t_ref[...] = (rows == cols).astype(f32)
-    row = lax.broadcasted_iota(jnp.int32, (size, 1), 0)
 
     def step(b, carry):
-        first = b * 8
-        for i in range(8):
-            at = first + i
-            line = a_ref[pl.ds(at, 1), :]
-            made = t_ref[pl.ds(at, 1), :]
-            pivot = line[:, i : i + 1]
-            scale = jnp.where(row > at, a_ref[:, i : i + 1] * (1.0 / pivot), 0.0)
-            scale = jnp.where(row == at, 1.0 - lax.rsqrt(pivot), scale)
-            a_ref[...] = a_ref[...] - scale * line
-            t_ref[...] = t_ref[...] - scale * made
-        a_ref[...] = pltpu.roll(a_ref[...], size - 8, 1)
+        first = pl.multiple_of(b * 8, 8)
+        line, made = a_ref[pl.ds(first, 8), :], t_ref[pl.ds(first, 8), :]
+        factors = panel_factor(pltpu.roll(line, lax.rem(size - first, size), 1))
+        line = functools.reduce(jnp.add, [f * spread(line[i : i + 1, :], 8) for i, f in enumerate(factors)])
+        made = functools.reduce(jnp.add, [f * spread(made[i : i + 1, :], 8) for i, f in enumerate(factors)])
+        t_ref[pl.ds(first, 8), :] = made
+        high, middle, low = thirds(jnp.concatenate([line, made], axis=1))
+        right = jnp.concatenate([high, middle, high, middle, low, high], axis=0)
+        left = jnp.concatenate([high, high, middle, middle, high, low], axis=0)[:, :size]
+        change = mm(left.astype(bf16), right.astype(bf16), TN)
+        a_ref[...] = a_ref[...] - change[:, :size]
+        t_ref[...] = t_ref[...] - jnp.where(rows >= first + 8, change[:, size:], 0.0)
         return carry
 
     lax.fori_loop(0, size // 8, step, 0)
@@ -276,7 +331,7 @@
     return k - g + shift * (rows == cols).astype(f32)
 
 
-def total_kernel(m_ref, q_ref, p_ref, o_ref, w_ref, core_ref, a_ref, t_ref, mine, *rest):
+def total_kernel(m_ref, q_ref, p_ref, o_ref, w_ref, core_ref, a_ref, t_ref, c_ref, mine, *rest):
     place = Place()
     greet(place)
     for k in range(2):
@@ -287,8 +342,10 @@
     total = rest[3]
     size = a_ref.shape[0]
 
+    def terms():
+        pivot_terms(q_ref, p_ref, core_ref)
+
     def first():
-        pivot_terms(q_ref, p_ref, core_ref)
         t0 = inverse_lower(shifted(core_ref[0, :size, :size], core_ref[1, :size, :size]), a_ref, t_ref)
         w_ref[:size, :size] = t0.T
         w_ref[size:, :size] = jnp.zeros((size, size), f32)
@@ -299,9 +356,12 @@
         g1 = core_ref[1, size:, size:] + exact(c10, c10, NT)
         t1 = inverse_lower(shifted(core_ref[0, size:, size:], g1), a_ref, t_ref)
         w_ref[size:, size:] = t1.T
-        w_ref[:size, size:] = -exact(turned, exact(t1, c10), NT)
-
-    device_sum(place, mine, *rest, first, second)
+        c_ref[...] = c10
+
+    def third():
+        w_ref[:size, size:] = -exact(w_ref[:size, :size], exact(t_ref[...], c_ref[...]), NT)
+
+    device_sum(place, mine, *rest, [terms, first, second, third])
     for k in range(2):
         for h in range(2):
             for j in range(6):
@@ -318,8 +378,7 @@
         out_specs=(pl.BlockSpec(memory_space=pltpu.VMEM),) * 2,
         scratch_shapes=[
             pltpu.VMEM((2, size, size), f32),
-            pltpu.VMEM((half, half), f32),
-            pltpu.VMEM((half, half), f32),
+            *[pltpu.VMEM((half, half), f32)] * 3,
             *sum_scratch(12),
         ],
         compiler_params=pltpu.CompilerParams(collective_id=1, has_side_effects=True, vmem_limit_bytes=40 * MB),
@@ -359,6 +418,7 @@
 
 
 def body(points, factor, pivots):
+    points = points.T
     q, p = fetch(points, factor, pivots)
     r, m = residual(points, factor, q, p)
     m, w = total_products(m, q, p)

time: 102 us -> 81 us (0.79)
  Pallas kernels: 95.2 us -> 78.2 us
  local copies, waits for them, and re-layouts: 5.88 us -> 1.9 us
    pallas_call x1, Pallas kernels: 38.3 us -> 24.6 us  [total_products(): pl.pallas_call(total_kernel, out_shape=(jax.ShapeDtypeStruct(m.shape, f32...]
    pallas_call x1, Pallas kernels: 22.3 us -> 17.3 us  [residual(): pl.pallas_call(residual_kernel, out_shape=(jax.ShapeDtypeStruct((count, s...]
    unnamed x5 -> x4, local copies, waits for them, and re-layouts: 5.88 us -> 1.9 us
    pallas_call x1, Pallas kernels: 27.8 us -> 29.6 us  [fetch(): pl.pallas_call(fetch_kernel, out_shape=(jax.ShapeDtypeStruct((256, 512),...]
where the time goes in v2:
time: 81 us; the launch traced here: 80.8 us
  Pallas kernels  78.2 us (97%)
  local copies, waits for them, and re-layouts  1.9 us (2%)
    pallas_call x1, Pallas kernels, fetch(): pl.pallas_call(fetch_kernel, out_shape=(jax.ShapeDtypeStruct((256, 512),...  29.6 us
    pallas_call x1, Pallas kernels, total_products(): pl.pallas_call(total_kernel, out_shape=(jax.ShapeDtypeStruct(m.shape, f32...  24.6 us
    pallas_call x1, Pallas kernels, residual(): pl.pallas_call(residual_kernel, out_shape=(jax.ShapeDtypeStruct((count, s...  17.3 us
    pallas_call x1, Pallas kernels, columns(): pl.pallas_call(functools.partial(columns_kernel, scale=1.0 / count), out_...  6.76 us
    unnamed x4, local copies, waits for them, and re-layouts  1.9 us

profile of v2, /device:TPU:1, one launch (start us, length us, event | category | flops | bytes accessed | tf_op | source)
XLA Modules:
  0.0 80.8 jit_solution(7402027083697025002)
XLA Ops:
  0.6 0.0 copy-start
  0.6 1.2 %copy-done = f32[4096,64]{0,1:T(8,128)S(1)} copy-done((f32[4096,64]{0,1:T(8,128)S(1)}, f32[4096,64]{0,1:T(8,128)}, u32[]{:S(2)}) %copy-start) | copy-done | bytes 1048600
  1.9 0.0 copy-start.1
  1.9 0.7 copy-done.1
  2.5 29.6 %shard_map.50 = (f32[256,512]{1,0:T(8,128)S(1)}, f32[128,128]{1,0:T(8,128)S(1)}) custom-call(s32[2,128]{1,0:T(2,128)S(1)} %copy-done.1, f32[64,4096]{1,0:T(8,128)S(1)} %bitcast.1, f32[4096,512]{1,0:T(8,128)} %factor.1), custom_call_target="tpu_custom_call" | custom-call | tf_op jit(solution)/shard_map/pallas_call | solution.py:163
  32.1 17.3 %shard_map.51 = (f32[4096,256]{1,0:T(8,128)S(1)}, f32[256,768]{1,0:T(8,128)S(1)}) custom-call(f32[64,4096]{1,0:T(8,128)S(1)} %bitcast.2, f32[4096,512]{1,0:T(8,128)} %factor.1, f32[256,512]{1,0:T(8,128)S(1)} %get-tuple-element.8.q_ref, f32[128,128]{1,0:T(8,128)S(1)} %get-tuple-element.9.p_ref), custom_call_target="tpu_custom_call" | custom-call | tf_op jit(solution)/shard_map/pallas_call | solution.py:229
  49.4 24.6 %shard_map.52 = (f32[256,768]{1,0:T(8,128)S(1)}, f32[256,256]{1,0:T(8,128)S(1)}) custom-call(f32[256,768]{1,0:T(8,128)S(1)} %get-tuple-element.11.m_ref, f32[256,512]{1,0:T(8,128)S(1)} %get-tuple-element.8.q_ref, f32[128,128]{1,0:T(8,128)S(1)} %get-tuple-element.9.p_ref), custom_call_target="tpu_custom_call" | custom-call | tf_op jit(solution)/shard_map/pallas_call | solution.py:374
  74.0 6.8 %shard_map.53 = (f32[4096,256]{1,0:T(8,128)}, f32[256,768]{1,0:T(8,128)}) custom-call(f32[4096,256]{1,0:T(8,128)S(1)} %get-tuple-element.10.r_ref, f32[256,256]{1,0:T(8,128)S(1)} %get-tuple-element.12.w_ref, f32[256,768]{1,0:T(8,128)S(1)} %get-tuple-element.13.m_ref), custom_call_target="tpu_custom_call" | custom-call | tf_op jit(solution)/shard_map/pallas_call | solution.py:405
Async XLA Ops:
  0.6 1.2 %copy-start = (f32[4096,64]{0,1:T(8,128)S(1)}, f32[4096,64]{0,1:T(8,128)}, u32[]{:S(2)}) copy-start(f32[4096,64]{0,1:T(8,128)} %param.3) | copy-start | bytes 3145732
  1.9 0.7 copy-start.1

commit v3 on v2

--- a/solution.py
+++ b/solution.py
@@ -32,11 +32,14 @@
     return high, (a - high.astype(f32)).astype(bf16)
 
 
-def offsets():
+PLANES = (2, 1, 3, 0)
+
+
+def offsets(plane):
     def hops(d):
-        return sum(min(c, 4 - c) for c in (d // 16, d // 4 % 4, d % 4))
-
-    return sorted(range(1, CHIPS), key=lambda d: (-hops(d), d))
+        return sum(min(c, 4 - c) for c in (d // 4, d % 4))
+
+    return sorted(range(0 if plane else 1, 16), key=lambda d: (-hops(d), d))
 
 
 class Place:
@@ -50,16 +53,21 @@
         zs = [(z + i) % 4 for i in range(4)]
         ys = [(y + i) % 4 for i in range(4)]
         xs = [(x + i) % 4 for i in range(4)]
-        self.peers = []
-        for d in offsets():
-            pz, pc = zs[d // 16], ys[d // 4 % 4] * 4 + xs[d % 4]
-            self.peers.append(((pz * 2 + self.core, pc), pz * 16 + pc))
+        self.ahead = [pl.multiple_of(z * 16, 16) for z in zs]
+        self.peers = {}
+        for plane in PLANES:
+            made = []
+            for d in offsets(plane):
+                at = ys[d // 4] * 4 + xs[d % 4]
+                made.append(((zs[plane] * 2 + self.core, at), zs[plane] * 16 + at))
+            self.peers[plane] = made
 
 
 def greet(place):
     barrier = pltpu.get_barrier_semaphore()
-    for device, _ in place.peers:
-        pl.semaphore_signal(barrier, inc=1, device_id=device, device_id_type=MESH)
+    for plane in PLANES:
+        for device, _ in place.peers[plane]:
+            pl.semaphore_signal(barrier, inc=1, device_id=device, device_id_type=MESH)
     pl.semaphore_signal(barrier, inc=1, device_id=place.other, device_id_type=MESH)
 
 
@@ -73,29 +81,45 @@
 
 def device_sum(place, mine, pair, arrived, own, total, send, recv, work=None):
     core, chip, other = place.core, place.chip, place.other
-    swap = remote(mine.at[1 - core], pair, send.at[0], recv.at[0], other)
     work = work or [lambda: None] * 4
-    swap.start()
+    swaps = {}
+    for plane in PLANES:
+        at = pl.ds(place.ahead[plane], 16)
+        swaps[plane] = remote(mine.at[1 - core, at], pair.at[at], send.at[plane], recv.at[plane], other)
+        swaps[plane].start()
     work[0]()
-    swap.wait_recv()
-    pair[...] = mine[core] + pair[...]
-    for slot, (device, target) in enumerate(place.peers):
-        remote(pair.at[target], arrived.at[slot], send.at[1], recv.at[1], device).start()
+    slot = 0
+    for plane in PLANES:
+        at = pl.ds(place.ahead[plane], 16)
+        swaps[plane].wait_recv()
+        pair[at] = mine[core, at] + pair[at]
+        for device, target in place.peers[plane]:
+            remote(pair.at[target], arrived.at[slot], send.at[4], recv.at[4], device).start()
+            slot += 1
     work[1]()
-    remote(arrived, arrived, send.at[1], recv.at[1], other).wait_recv()
+    remote(arrived, arrived, send.at[4], recv.at[4], other).wait_recv()
     own[...] = pair[chip] + jnp.sum(arrived[...], axis=0)
-    for device, _ in place.peers:
-        remote(own, total.at[core, chip], send.at[2], recv.at[2], device).start()
+    for plane in PLANES:
+        for device, _ in place.peers[plane]:
+            remote(own, total.at[core, chip], send.at[5 + plane], recv.at[5 + plane], device).start()
     total[core, chip] = own[...]
     work[2]()
-    remote(arrived, arrived, send.at[2], recv.at[2], other).wait_recv()
-    back = remote(total.at[core], total.at[core], send.at[3], recv.at[3], other)
-    back.start()
+    backs = []
+    for plane in reversed(PLANES):
+        some = arrived.at[pl.ds(0, 16 if plane else 15)]
+        remote(some, some, send.at[5 + plane], recv.at[5 + plane], other).wait_recv()
+        block = total.at[core, pl.ds(place.ahead[-plane % 4], 16)]
+        backs.append(remote(block, block, send.at[9 + plane], recv.at[9 + plane], other))
+        backs[-1].start()
     work[3]()
-    swap.wait_send()
-    remote(arrived, arrived, send.at[1], recv.at[1], other).wait_send()
-    remote(arrived, arrived, send.at[2], recv.at[2], other).wait_send()
-    back.wait()
+    for plane in PLANES:
+        swaps[plane].wait_send()
+    remote(arrived, arrived, send.at[4], recv.at[4], other).wait_send()
+    for plane in PLANES:
+        some = arrived.at[pl.ds(0, 16 if plane else 15)]
+        remote(some, some, send.at[5 + plane], recv.at[5 + plane], other).wait_send()
+    for back in backs:
+        back.wait()
 
 
 def sum_scratch(rows):
@@ -105,8 +129,8 @@
         pltpu.VMEM((CHIPS - 1, rows, 128), f32),
         pltpu.VMEM((rows, 128), f32),
         pltpu.VMEM((2, CHIPS, rows, 128), f32),
-        pltpu.SemaphoreType.DMA((4,)),
-        pltpu.SemaphoreType.DMA((4,)),
+        pltpu.SemaphoreType.DMA((13,)),
+        pltpu.SemaphoreType.DMA((13,)),
     ]
 
 
@@ -177,7 +201,7 @@
     )(pivots, points, factor)
 
 
-def residual_kernel(points, factor, q_ref, p_ref, r_ref, m_ref, qh, ql, pt, pn, cross, xa, ra, xb, rb):
+def residual_kernel(points, factor, q_ref, p_ref, r_ref, m_ref, qh, ql, pt, pn, turned, cross, xa, ra, xb, rb):
     step = pl.program_id(0)
     width = points.shape[0]
     tile, wide = factor.shape[0] // 2, factor.shape[1]
@@ -190,7 +214,7 @@
         high, low = halves(p)
         pt[...] = jnp.concatenate([high, low, high, low], axis=0)
         pn[...] = jnp.sum(p * p, axis=0, keepdims=True) * (width / 4.0)
-        for ref in (m_ref, cross, xb, rb):
+        for ref in (turned, cross, xb, rb):
             ref[...] = jnp.zeros_like(ref)
 
     def make(first, x, r):
@@ -207,9 +231,11 @@
 
     def add(x, r):
         rh, rl = r[0], r[1]
-        m_ref[:, :wide] += mm(rh, x[0], TN) + mm(rh, x[1], TN) + mm(rl, x[0], TN)
-        m_ref[:, wide:] += mm(rh, rh, TN)
-        cross[...] += mm(rh, rl, TN)
+        size = rh.shape[1]
+        both = mm(jnp.concatenate([x[0], x[1], rh, rl], axis=1), rh, TN)
+        turned[:wide, :] += both[:wide] + both[wide : 2 * wide] + mm(x[0], rl, TN)
+        turned[wide:, :] += both[2 * wide : 2 * wide + size]
+        cross[...] += both[2 * wide + size :]
 
     add(xb, rb)
     make(0, xa, ra)
@@ -219,10 +245,11 @@
     @pl.when(step == pl.num_programs(0) - 1)
     def _():
         add(xb, rb)
-        m_ref[:, wide:] += cross[...] + cross[...].T
-
-
-def residual(points, factor, q, p, tile=512):
+        m_ref[:, :wide] = turned[:wide, :].T
+        m_ref[:, wide:] = turned[wide:, :] + cross[...] + cross[...].T
+
+
+def residual(points, factor, q, p, tile=1024):
     width, count = points.shape
     wide = factor.shape[1]
     size = q.shape[0]
@@ -245,6 +272,7 @@
             pltpu.VMEM((wide, size), bf16),
             pltpu.VMEM((4 * width, size), bf16),
             pltpu.VMEM((1, size), f32),
+            pltpu.VMEM((wide + size, size), f32),
             pltpu.VMEM((size, size), f32),
             *[pltpu.VMEM((2, tile // 2, wide), bf16), pltpu.VMEM((2, tile // 2, size), bf16)] * 2,
         ],
@@ -287,12 +315,16 @@
     return high, middle, a - high - middle
 
 
-def inverse_lower(core, a_ref, t_ref):
-    size = core.shape[0]
-    rows = lax.broadcasted_iota(jnp.int32, (size, size), 0)
-    cols = lax.broadcasted_iota(jnp.int32, (size, size), 1)
+def begin_inverse(core, a_ref, t_ref):
+    rows = lax.broadcasted_iota(jnp.int32, core.shape, 0)
+    cols = lax.broadcasted_iota(jnp.int32, core.shape, 1)
     a_ref[...] = core
     t_ref[...] = (rows == cols).astype(f32)
+
+
+def run_inverse(a_ref, t_ref, start, stop):
+    size = a_ref.shape[0]
+    rows = lax.broadcasted_iota(jnp.int32, (size, size), 0)
 
     def step(b, carry):
         first = pl.multiple_of(b * 8, 8)
@@ -309,8 +341,7 @@
         t_ref[...] = t_ref[...] - jnp.where(rows >= first + 8, change[:, size:], 0.0)
         return carry
 
-    lax.fori_loop(0, size // 8, step, 0)
-    return t_ref[...]
+    lax.fori_loop(start, stop, step, 0)
 
 
 def pivot_terms(q_ref, p_ref, core_ref):
@@ -342,26 +373,31 @@
     total = rest[3]
     size = a_ref.shape[0]
 
-    def terms():
+    def during_swap():
         pivot_terms(q_ref, p_ref, core_ref)
-
-    def first():
-        t0 = inverse_lower(shifted(core_ref[0, :size, :size], core_ref[1, :size, :size]), a_ref, t_ref)
-        w_ref[:size, :size] = t0.T
+        begin_inverse(shifted(core_ref[0, :size, :size], core_ref[1, :size, :size]), a_ref, t_ref)
+
+    def during_scatter():
+        run_inverse(a_ref, t_ref, 0, 12)
+
+    def during_gather():
+        run_inverse(a_ref, t_ref, 12, 16)
+        turned = t_ref[...].T
+        w_ref[:size, :size] = turned
         w_ref[size:, :size] = jnp.zeros((size, size), f32)
-
-    def second():
-        turned = w_ref[:size, :size]
         c10 = exact(core_ref[0, size:, :size] - core_ref[1, size:, :size], turned)
+        c_ref[...] = c10
         g1 = core_ref[1, size:, size:] + exact(c10, c10, NT)
-        t1 = inverse_lower(shifted(core_ref[0, size:, size:], g1), a_ref, t_ref)
+        begin_inverse(shifted(core_ref[0, size:, size:], g1), a_ref, t_ref)
+        run_inverse(a_ref, t_ref, 0, 8)
+
+    def on_the_way_back():
+        run_inverse(a_ref, t_ref, 8, 16)
+        t1 = t_ref[...]
         w_ref[size:, size:] = t1.T
-        c_ref[...] = c10
-
-    def third():
-        w_ref[:size, size:] = -exact(w_ref[:size, :size], exact(t_ref[...], c_ref[...]), NT)
-
-    device_sum(place, mine, *rest, [terms, first, second, third])
+        w_ref[:size, size:] = -exact(w_ref[:size, :size], exact(t1, c_ref[...]), NT)
+
+    device_sum(place, mine, *rest, [during_swap, during_scatter, during_gather, on_the_way_back])
     for k in range(2):
         for h in range(2):
             for j in range(6):
@@ -385,22 +421,26 @@
     )(m, q, p)
 
 
-def columns_kernel(r_ref, w_ref, m_ref, c_ref, g_ref, wh, wl, *, scale):
-    @pl.when(pl.program_id(0) == 0)
+def product(a, b):
+    ah, al = halves(a)
+    bh, bl = halves(b)
+    both = mm(jnp.concatenate([ah, al], axis=0), bh)
+    return both[: len(a)] + both[len(a) :] + mm(ah, bl)
+
+
+def columns_kernel(r_ref, w_ref, m_ref, c_ref, g_ref, *, scale):
+    w = w_ref[...]
+    c_ref[...] = product(r_ref[...], w)
+
+    @pl.when(pl.program_id(0) == pl.num_programs(0) - 1)
     def _():
-        w = w_ref[...]
-        wh[...], wl[...] = halves(w)
         size = w.shape[0]
         wide = m_ref.shape[1] - size
-        turned = w.T
-        g_ref[:, :wide] = exact(turned, m_ref[:, :wide]) * scale
-        g_ref[:, wide:] = exact(turned, exact(m_ref[:, wide:], w)) * scale
-
-    rh, rl = halves(r_ref[...])
-    c_ref[...] = mm(rh, wh[...]) + mm(rh, wl[...]) + mm(rl, wh[...])
-
-
-def columns(r, w, m, tile=512):
+        right = product(m_ref[:, wide:], w)
+        g_ref[...] = product(w.T, jnp.concatenate([m_ref[:, :wide], right], axis=1)) * scale
+
+
+def columns(r, w, m, tile=1024):
     count, size = r.shape
     return pl.pallas_call(
         functools.partial(columns_kernel, scale=1.0 / count),
@@ -412,7 +452,6 @@
             pl.BlockSpec(m.shape, lambda i: (0, 0)),
         ],
         out_specs=(pl.BlockSpec((tile, size), lambda i: (i, 0)), pl.BlockSpec(m.shape, lambda i: (0, 0))),
-        scratch_shapes=[pltpu.VMEM(w.shape, bf16)] * 2,
         compiler_params=pltpu.CompilerParams(vmem_limit_bytes=40 * MB),
     )(r, w, m)
 

time: 81 us -> 73.9 us (0.912)
  Pallas kernels: 78.2 us -> 70.6 us
    pallas_call x1, Pallas kernels: 17.3 us -> 13 us  [residual(): pl.pallas_call(residual_kernel, out_shape=(jax.ShapeDtypeStruct((count, s...]
    pallas_call x1, Pallas kernels: 6.76 us -> 4.65 us  [columns(): pl.pallas_call(functools.partial(columns_kernel, scale=1.0 / count), out_...]
    pallas_call x1, Pallas kernels: 29.6 us -> 28.7 us  [fetch(): pl.pallas_call(fetch_kernel, out_shape=(jax.ShapeDtypeStruct((256, 512),...]
where the time goes in v3:
time: 73.9 us; the launch traced here: 73.2 us
  Pallas kernels  70.6 us (96%)
  local copies, waits for them, and re-layouts  1.9 us (3%)
    pallas_call x1, Pallas kernels, fetch(): pl.pallas_call(fetch_kernel, out_shape=(jax.ShapeDtypeStruct((256, 512),...  28.7 us
    pallas_call x1, Pallas kernels, total_products(): pl.pallas_call(total_kernel, out_shape=(jax.ShapeDtypeStruct(m.shape, f32...  24.3 us
    pallas_call x1, Pallas kernels, residual(): pl.pallas_call(residual_kernel, out_shape=(jax.ShapeDtypeStruct((count, s...  13 us
    pallas_call x1, Pallas kernels, columns(): pl.pallas_call(functools.partial(columns_kernel, scale=1.0 / count), out_...  4.65 us
    unnamed x4, local copies, waits for them, and re-layouts  1.9 us

profile of v3, /device:TPU:1, one launch (start us, length us, event | category | flops | bytes accessed | tf_op | source)
XLA Modules:
  0.0 73.2 jit_solution(10470035872548338369)
XLA Ops:
  0.6 0.0 copy-start
  0.6 1.2 %copy-done = f32[4096,64]{0,1:T(8,128)S(1)} copy-done((f32[4096,64]{0,1:T(8,128)S(1)}, f32[4096,64]{0,1:T(8,128)}, u32[]{:S(2)}) %copy-start) | copy-done | bytes 1048600
  1.9 0.0 copy-start.1
  1.9 0.7 copy-done.1
  2.5 28.7 %shard_map.50 = (f32[256,512]{1,0:T(8,128)S(1)}, f32[128,128]{1,0:T(8,128)S(1)}) custom-call(s32[2,128]{1,0:T(2,128)S(1)} %copy-done.1, f32[64,4096]{1,0:T(8,128)S(1)} %bitcast.1, f32[4096,512]{1,0:T(8,128)} %factor.1), custom_call_target="tpu_custom_call" | custom-call | tf_op jit(solution)/shard_map/pallas_call | solution.py:187
  31.2 13.0 %shard_map.51 = (f32[4096,256]{1,0:T(8,128)S(1)}, f32[256,768]{1,0:T(8,128)S(1)}) custom-call(f32[64,4096]{1,0:T(8,128)S(1)} %bitcast.2, f32[4096,512]{1,0:T(8,128)} %factor.1, f32[256,512]{1,0:T(8,128)S(1)} %get-tuple-element.8.q_ref, f32[128,128]{1,0:T(8,128)S(1)} %get-tuple-element.9.p_ref), custom_call_target="tpu_custom_call" | custom-call | tf_op jit(solution)/shard_map/pallas_call | solution.py:256
  44.2 24.3 %shard_map.52 = (f32[256,768]{1,0:T(8,128)S(1)}, f32[256,256]{1,0:T(8,128)S(1)}) custom-call(f32[256,768]{1,0:T(8,128)S(1)} %get-tuple-element.11.m_ref, f32[256,512]{1,0:T(8,128)S(1)} %get-tuple-element.8.q_ref, f32[128,128]{1,0:T(8,128)S(1)} %get-tuple-element.9.p_ref), custom_call_target="tpu_custom_call" | custom-call | tf_op jit(solution)/shard_map/pallas_call | solution.py:410
  68.5 4.7 %shard_map.53 = (f32[4096,256]{1,0:T(8,128)}, f32[256,768]{1,0:T(8,128)}) custom-call(f32[4096,256]{1,0:T(8,128)S(1)} %get-tuple-element.10.r_ref, f32[256,256]{1,0:T(8,128)S(1)} %get-tuple-element.12.w_ref, f32[256,768]{1,0:T(8,128)S(1)} %get-tuple-element.13.m_ref), custom_call_target="tpu_custom_call" | custom-call | tf_op jit(solution)/shard_map/pallas_call | solution.py:445
Async XLA Ops:
  0.6 1.2 %copy-start = (f32[4096,64]{0,1:T(8,128)S(1)}, f32[4096,64]{0,1:T(8,128)}, u32[]{:S(2)}) copy-start(f32[4096,64]{0,1:T(8,128)} %param.3) | copy-start | bytes 3145732
  1.9 0.7 copy-start.1

commit v4 on v3

--- a/solution.py
+++ b/solution.py
@@ -132,152 +132,6 @@
         pltpu.SemaphoreType.DMA((13,)),
         pltpu.SemaphoreType.DMA((13,)),
     ]
-
-
-def fetch_kernel(pivots_hbm, points_hbm, factor_hbm, q_ref, p_ref, pivots, turned, points, factor, load, mine, *rest):
-    place = Place()
-    loads = [
-        pltpu.make_async_copy(points_hbm, turned, load.at[0]),
-        pltpu.make_async_copy(pivots_hbm, pivots, load.at[1]),
-        pltpu.make_async_copy(factor_hbm, factor, load.at[2]),
-    ]
-    for copy in loads:
-        copy.start()
-    greet(place)
-    count = points.shape[0]
-    first = place.number * count
-    loads[0].wait()
-
-    def turn(i, carry):
-        at = pl.multiple_of(i * 128, 128)
-        points[pl.ds(at, 128), :] = turned[:, pl.ds(at, 128)].T
-        return carry
-
-    lax.fori_loop(0, count // 128, turn, 0)
-    loads[1].wait()
-    loads[2].wait()
-
-    def pick(i, carry):
-        rows = []
-        for s in range(2):
-            local = pivots[s, i] - first
-            inside = ((local >= 0) & (local < count)).astype(jnp.int32).astype(f32)
-            local = jnp.clip(local, 0, count - 1)
-            rows.append((points[pl.ds(local, 1), :] * inside, factor[pl.ds(local, 1), :] * inside))
-        half, chip = i // CHIPS, i % CHIPS
-        for s in range(2):
-            for j in range(4):
-                mine[half, chip, pl.ds(4 * s + j, 1), :] = rows[s][1][:, 128 * j : 128 * (j + 1)]
-        mine[half, chip, pl.ds(8, 1), :] = jnp.concatenate([rows[0][0], rows[1][0]], axis=1)
-        return carry
-
-    lax.fori_loop(0, 2 * CHIPS, pick, 0, unroll=4)
-    greeted()
-    total = rest[3]
-    device_sum(place, mine, *rest)
-    for half in range(2):
-        for s in range(2):
-            for j in range(4):
-                q_ref[pl.ds(128 * s + CHIPS * half, CHIPS), pl.ds(128 * j, 128)] = total[half, :, 4 * s + j, :]
-        p_ref[pl.ds(CHIPS * half, CHIPS), :] = total[half, :, 8, :]
-
-
-def fetch(points, factor, pivots):
-    width, count = points.shape
-    return pl.pallas_call(
-        fetch_kernel,
-        out_shape=(jax.ShapeDtypeStruct((256, 512), f32), jax.ShapeDtypeStruct((128, 128), f32)),
-        in_specs=[pl.BlockSpec(memory_space=pltpu.HBM)] * 3,
-        out_specs=(pl.BlockSpec(memory_space=pltpu.VMEM), pl.BlockSpec(memory_space=pltpu.VMEM)),
-        scratch_shapes=[
-            pltpu.SMEM(pivots.shape, jnp.int32),
-            pltpu.VMEM((width, count), f32),
-            pltpu.VMEM((count, width), f32),
-            pltpu.VMEM(factor.shape, f32),
-            pltpu.SemaphoreType.DMA((3,)),
-            *sum_scratch(9),
-        ],
-        compiler_params=pltpu.CompilerParams(collective_id=0, has_side_effects=True, vmem_limit_bytes=51 * MB),
-    )(pivots, points, factor)
-
-
-def residual_kernel(points, factor, q_ref, p_ref, r_ref, m_ref, qh, ql, pt, pn, turned, cross, xa, ra, xb, rb):
-    step = pl.program_id(0)
-    width = points.shape[0]
-    tile, wide = factor.shape[0] // 2, factor.shape[1]
-
-    @pl.when(step == 0)
-    def _():
-        qh[...], ql[...] = halves(q_ref[...].T)
-        pp = p_ref[...].T
-        p = jnp.concatenate([pp[:width], pp[width:]], axis=1) * (2.0 / width)
-        high, low = halves(p)
-        pt[...] = jnp.concatenate([high, low, high, low], axis=0)
-        pn[...] = jnp.sum(p * p, axis=0, keepdims=True) * (width / 4.0)
-        for ref in (turned, cross, xb, rb):
-            ref[...] = jnp.zeros_like(ref)
-
-    def make(first, x, r):
-        a = points[:, first : first + tile]
-        high, low = halves(a)
-        inner = mm(jnp.concatenate([high, high, low, low], axis=0), pt[...], TN)
-        norm = jnp.sum(a * a, axis=0, keepdims=True) * (1.0 / width)
-        norm = jnp.broadcast_to(norm, (8, tile)).T[:, :1]
-        xh, xl = halves(factor[first : first + tile, :])
-        value = jnp.exp(inner - norm - pn[...]) - (mm(xh, qh[...]) + mm(xh, ql[...]) + mm(xl, qh[...]))
-        r_ref[first : first + tile, :] = value
-        x[0], x[1] = xh, xl
-        r[0], r[1] = halves(value)
-
-    def add(x, r):
-        rh, rl = r[0], r[1]
-        size = rh.shape[1]
-        both = mm(jnp.concatenate([x[0], x[1], rh, rl], axis=1), rh, TN)
-        turned[:wide, :] += both[:wide] + both[wide : 2 * wide] + mm(x[0], rl, TN)
-        turned[wide:, :] += both[2 * wide : 2 * wide + size]
-        cross[...] += both[2 * wide + size :]
-
-    add(xb, rb)
-    make(0, xa, ra)
-    add(xa, ra)
-    make(tile, xb, rb)
-
-    @pl.when(step == pl.num_programs(0) - 1)
-    def _():
-        add(xb, rb)
-        m_ref[:, :wide] = turned[:wide, :].T
-        m_ref[:, wide:] = turned[wide:, :] + cross[...] + cross[...].T
-
-
-def residual(points, factor, q, p, tile=1024):
-    width, count = points.shape
-    wide = factor.shape[1]
-    size = q.shape[0]
-    return pl.pallas_call(
-        residual_kernel,
-        out_shape=(jax.ShapeDtypeStruct((count, size), f32), jax.ShapeDtypeStruct((size, wide + size), f32)),
-        grid=(count // tile,),
-        in_specs=[
-            pl.BlockSpec((width, tile), lambda i: (0, i)),
-            pl.BlockSpec((tile, wide), lambda i: (i, 0)),
-            pl.BlockSpec(q.shape, lambda i: (0, 0)),
-            pl.BlockSpec(p.shape, lambda i: (0, 0)),
-        ],
-        out_specs=(
-            pl.BlockSpec((tile, size), lambda i: (i, 0)),
-            pl.BlockSpec((size, wide + size), lambda i: (0, 0)),
-        ),
-        scratch_shapes=[
-            pltpu.VMEM((wide, size), bf16),
-            pltpu.VMEM((wide, size), bf16),
-            pltpu.VMEM((4 * width, size), bf16),
-            pltpu.VMEM((1, size), f32),
-            pltpu.VMEM((wide + size, size), f32),
-            pltpu.VMEM((size, size), f32),
-            *[pltpu.VMEM((2, tile // 2, wide), bf16), pltpu.VMEM((2, tile // 2, size), bf16)] * 2,
-        ],
-        compiler_params=pltpu.CompilerParams(vmem_limit_bytes=40 * MB),
-    )(points, factor, q, p)
 
 
 def spread(a, rows):
@@ -362,15 +216,111 @@
     return k - g + shift * (rows == cols).astype(f32)
 
 
-def total_kernel(m_ref, q_ref, p_ref, o_ref, w_ref, core_ref, a_ref, t_ref, c_ref, mine, *rest):
+def load_rows(place, pivots, turned, points, factor, mine, loads):
+    count, width = points.shape
+    first = place.number * count
+    loads[0].wait()
+
+    def turn(i, carry):
+        at = pl.multiple_of(i * 128, 128)
+        points[pl.ds(at, 128), :] = turned[:, pl.ds(at, 128)].T
+        return carry
+
+    lax.fori_loop(0, count // 128, turn, 0)
+    loads[1].wait()
+    loads[2].wait()
+
+    def pick(i, carry):
+        rows = []
+        for s in range(2):
+            local = pivots[s, i] - first
+            inside = ((local >= 0) & (local < count)).astype(jnp.int32).astype(f32)
+            local = jnp.clip(local, 0, count - 1)
+            rows.append((points[pl.ds(local, 1), :] * inside, factor[pl.ds(local, 1), :] * inside))
+        half, chip = i // CHIPS, i % CHIPS
+        for s in range(2):
+            for j in range(4):
+                mine[half, chip, pl.ds(4 * s + j, 1), :] = rows[s][1][:, 128 * j : 128 * (j + 1)]
+        mine[half, chip, pl.ds(8, 1), :] = jnp.concatenate([rows[0][0], rows[1][0]], axis=1)
+        return carry
+
+    lax.fori_loop(0, 2 * CHIPS, pick, 0, unroll=4)
+
+
+def residual(turned, factor, q_ref, p_ref, r_ref, m_ref, qh, ql, pt, pn, flipped, cross, xa, ra, xb, rb):
+    width, count = turned.shape
+    tile, wide = xa.shape[1:]
+    qh[...], ql[...] = halves(q_ref[...].T)
+    pp = p_ref[...].T
+    p = jnp.concatenate([pp[:width], pp[width:]], axis=1) * (2.0 / width)
+    high, low = halves(p)
+    pt[...] = jnp.concatenate([high, low, high, low], axis=0)
+    pn[...] = jnp.sum(p * p, axis=0, keepdims=True) * (width / 4.0)
+    for ref in (flipped, cross, xb, rb):
+        ref[...] = jnp.zeros_like(ref)
+
+    def make(first, x, r):
+        first = pl.multiple_of(first, tile)
+        a = turned[:, pl.ds(first, tile)]
+        high, low = halves(a)
+        inner = mm(jnp.concatenate([high, high, low, low], axis=0), pt[...], TN)
+        norm = jnp.sum(a * a, axis=0, keepdims=True) * (1.0 / width)
+        norm = jnp.broadcast_to(norm, (8, tile)).T[:, :1]
+        xh, xl = halves(factor[pl.ds(first, tile), :])
+        value = jnp.exp(inner - norm - pn[...]) - (mm(xh, qh[...]) + mm(xh, ql[...]) + mm(xl, qh[...]))
+        r_ref[pl.ds(first, tile), :] = value
+        x[0], x[1] = xh, xl
+        r[0], r[1] = halves(value)
+
+    def add(x, r):
+        rh, rl = r[0], r[1]
+        size = rh.shape[1]
+        both = mm(jnp.concatenate([x[0], x[1], rh, rl], axis=1), rh, TN)
+        flipped[:wide, :] += both[:wide] + both[wide : 2 * wide] + mm(x[0], rl, TN)
+        flipped[wide:, :] += both[2 * wide : 2 * wide + size]
+        cross[...] += both[2 * wide + size :]
+
+    def step(i, carry):
+        add(xb, rb)
+        make(2 * i * tile, xa, ra)
+        add(xa, ra)
+        make((2 * i + 1) * tile, xb, rb)
+        return carry
+
+    lax.fori_loop(0, count // (2 * tile), step, 0)
+    add(xb, rb)
+    m_ref[:, :wide] = flipped[:wide, :].T
+    m_ref[:, wide:] = flipped[wide:, :] + cross[...] + cross[...].T
+
+
+def main_kernel(pivots_hbm, points_hbm, factor_hbm, r_ref, m_ref, w_ref, pivots, turned, points, factor, load, *rest):
     place = Place()
+    loads = [
+        pltpu.make_async_copy(points_hbm, turned, load.at[0]),
+        pltpu.make_async_copy(pivots_hbm, pivots, load.at[1]),
+        pltpu.make_async_copy(factor_hbm, factor, load.at[2]),
+    ]
+    for copy in loads:
+        copy.start()
     greet(place)
+    rest = list(rest)
+    sum_a, sum_b, rest = rest[:7], rest[7:14], rest[14:]
+    q_ref, p_ref, core_ref, a_ref, t_ref, c_ref, *rest = rest
+    load_rows(place, pivots, turned, points, factor, sum_a[0], loads)
+    greeted()
+    device_sum(place, *sum_a)
+    total = sum_a[4]
+    for half in range(2):
+        for s in range(2):
+            for j in range(4):
+                q_ref[pl.ds(128 * s + CHIPS * half, CHIPS), pl.ds(128 * j, 128)] = total[half, :, 4 * s + j, :]
+        p_ref[pl.ds(CHIPS * half, CHIPS), :] = total[half, :, 8, :]
+
+    residual(turned, factor, q_ref, p_ref, r_ref, m_ref, *rest)
     for k in range(2):
         for h in range(2):
             for j in range(6):
-                mine[k, :, 2 * j + h, :] = m_ref[pl.ds(128 * k + CHIPS * h, CHIPS), pl.ds(128 * j, 128)]
-    greeted()
-    total = rest[3]
+                sum_b[0][k, :, 2 * j + h, :] = m_ref[pl.ds(128 * k + CHIPS * h, CHIPS), pl.ds(128 * j, 128)]
     size = a_ref.shape[0]
 
     def during_swap():
@@ -397,28 +347,50 @@
         w_ref[size:, size:] = t1.T
         w_ref[:size, size:] = -exact(w_ref[:size, :size], exact(t1, c_ref[...]), NT)
 
-    device_sum(place, mine, *rest, [during_swap, during_scatter, during_gather, on_the_way_back])
+    device_sum(place, *sum_b, [during_swap, during_scatter, during_gather, on_the_way_back])
+    total = sum_b[4]
     for k in range(2):
         for h in range(2):
             for j in range(6):
-                o_ref[pl.ds(128 * k + CHIPS * h, CHIPS), pl.ds(128 * j, 128)] = total[k, :, 2 * j + h, :]
-
-
-def total_products(m, q, p):
-    size = q.shape[0]
-    half = size // 2
+                m_ref[pl.ds(128 * k + CHIPS * h, CHIPS), pl.ds(128 * j, 128)] = total[k, :, 2 * j + h, :]
+
+
+def main(points, factor, pivots, tile=512):
+    width, count = points.shape
+    wide = factor.shape[1]
+    blocks, half = pivots.shape
+    size = blocks * half
     return pl.pallas_call(
-        total_kernel,
-        out_shape=(jax.ShapeDtypeStruct(m.shape, f32), jax.ShapeDtypeStruct((size, size), f32)),
-        in_specs=[pl.BlockSpec(memory_space=pltpu.VMEM)] * 3,
-        out_specs=(pl.BlockSpec(memory_space=pltpu.VMEM),) * 2,
+        main_kernel,
+        out_shape=(
+            jax.ShapeDtypeStruct((count, size), f32),
+            jax.ShapeDtypeStruct((size, wide + size), f32),
+            jax.ShapeDtypeStruct((size, size), f32),
+        ),
+        in_specs=[pl.BlockSpec(memory_space=pltpu.HBM)] * 3,
+        out_specs=(pl.BlockSpec(memory_space=pltpu.VMEM),) * 3,
         scratch_shapes=[
+            pltpu.SMEM(pivots.shape, jnp.int32),
+            pltpu.VMEM((width, count), f32),
+            pltpu.VMEM((count, width), f32),
+            pltpu.VMEM(factor.shape, f32),
+            pltpu.SemaphoreType.DMA((3,)),
+            *sum_scratch(9),
+            *sum_scratch(12),
+            pltpu.VMEM((size, wide), f32),
+            pltpu.VMEM((half, 2 * width), f32),
             pltpu.VMEM((2, size, size), f32),
             *[pltpu.VMEM((half, half), f32)] * 3,
-            *sum_scratch(12),
+            pltpu.VMEM((wide, size), bf16),
+            pltpu.VMEM((wide, size), bf16),
+            pltpu.VMEM((4 * width, size), bf16),
+            pltpu.VMEM((1, size), f32),
+            pltpu.VMEM((wide + size, size), f32),
+            pltpu.VMEM((size, size), f32),
+            *[pltpu.VMEM((2, tile, wide), bf16), pltpu.VMEM((2, tile, size), bf16)] * 2,
         ],
-        compiler_params=pltpu.CompilerParams(collective_id=1, has_side_effects=True, vmem_limit_bytes=40 * MB),
-    )(m, q, p)
+        compiler_params=pltpu.CompilerParams(collective_id=0, has_side_effects=True, vmem_limit_bytes=44 * MB),
+    )(pivots, points, factor)
 
 
 def product(a, b):
@@ -436,8 +408,9 @@
     def _():
         size = w.shape[0]
         wide = m_ref.shape[1] - size
-        right = product(m_ref[:, wide:], w)
-        g_ref[...] = product(w.T, jnp.concatenate([m_ref[:, :wide], right], axis=1)) * scale
+        turned = w.T
+        g_ref[:, :wide] = exact(turned, m_ref[:, :wide]) * scale
+        g_ref[:, wide:] = exact(turned, exact(m_ref[:, wide:], w)) * scale
 
 
 def columns(r, w, m, tile=1024):
@@ -458,9 +431,7 @@
 
 def body(points, factor, pivots):
     points = points.T
-    q, p = fetch(points, factor, pivots)
-    r, m = residual(points, factor, q, p)
-    m, w = total_products(m, q, p)
+    r, m, w = main(points, factor, pivots)
     return columns(r, w, m)
 
 

time: 73.9 us -> 70.1 us (0.949)
  Pallas kernels: 70.6 us -> 67.4 us
    pallas_call x3 -> x1, Pallas kernels: 66 us -> 61.8 us  [main(): pl.pallas_call(main_kernel, out_shape=(jax.ShapeDtypeStruct((count, size)...]
    pallas_call x1, Pallas kernels: 4.65 us -> 5.59 us  [columns(): pl.pallas_call(functools.partial(columns_kernel, scale=1.0 / count), out_...]
where the time goes in v4:
time: 70.1 us; the launch traced here: 69.9 us
  Pallas kernels  67.4 us (96%)
  local copies, waits for them, and re-layouts  1.9 us (3%)
    pallas_call x1, Pallas kernels, main(): pl.pallas_call(main_kernel, out_shape=(jax.ShapeDtypeStruct((count, size)...  61.8 us
    pallas_call x1, Pallas kernels, columns(): pl.pallas_call(functools.partial(columns_kernel, scale=1.0 / count), out_...  5.59 us
    unnamed x4, local copies, waits for them, and re-layouts  1.9 us

profile of v4, /device:TPU:1, one launch (start us, length us, event | category | flops | bytes accessed | tf_op | source)
XLA Modules:
  0.0 69.9 jit_solution(6516666608049677431)
XLA Ops:
  0.6 0.0 copy-start
  0.6 1.2 %copy-done = f32[4096,64]{0,1:T(8,128)S(1)} copy-done((f32[4096,64]{0,1:T(8,128)S(1)}, f32[4096,64]{0,1:T(8,128)}, u32[]{:S(2)}) %copy-start) | copy-done | bytes 1048600
  1.9 0.0 copy-start.1
  1.9 0.7 copy-done.1
  2.5 61.8 %shard_map.50 = (f32[4096,256]{1,0:T(8,128)S(1)}, f32[256,768]{1,0:T(8,128)S(1)}, f32[256,256]{1,0:T(8,128)S(1)}) custom-call(s32[2,128]{1,0:T(2,128)S(1)} %copy-done.1, f32[64,4096]{1,0:T(8,128)S(1)} %bitcast.1, f32[4096,512]{1,0:T(8,128)} %factor_hbm.1), custom_call_target="tpu_custom_call" | custom-call | tf_op jit(solution)/shard_map/pallas_call | solution.py:363
  64.4 5.6 %shard_map.51 = (f32[4096,256]{1,0:T(8,128)}, f32[256,768]{1,0:T(8,128)}) custom-call(f32[4096,256]{1,0:T(8,128)S(1)} %get-tuple-element.5.r_ref, f32[256,256]{1,0:T(8,128)S(1)} %get-tuple-element.6.w_ref, f32[256,768]{1,0:T(8,128)S(1)} %get-tuple-element.7.m_ref), custom_call_target="tpu_custom_call" | custom-call | tf_op jit(solution)/shard_map/pallas_call | solution.py:418
Async XLA Ops:
  0.6 1.2 %copy-start = (f32[4096,64]{0,1:T(8,128)S(1)}, f32[4096,64]{0,1:T(8,128)}, u32[]{:S(2)}) copy-start(f32[4096,64]{0,1:T(8,128)} %param.3) | copy-start | bytes 3145732
  1.9 0.7 copy-start.1

commit v5 on v4

--- a/solution.py
+++ b/solution.py
@@ -160,7 +160,7 @@
         for i in range(j, 8):
             column = jnp.where(row == i, inverse[i, j], column)
         made.append(column)
-    return made
+    return made, inverse
 
 
 def thirds(a):
@@ -169,30 +169,46 @@
     return high, middle, a - high - middle
 
 
-def begin_inverse(core, a_ref, t_ref):
+def weighed(factors, rows):
+    return functools.reduce(jnp.add, [f * spread(rows[i : i + 1, :], 8) for i, f in enumerate(factors)])
+
+
+def begin_inverse(core, state):
+    a_ref, t_ref, panel_ref, left_ref, right_ref = state
     rows = lax.broadcasted_iota(jnp.int32, core.shape, 0)
     cols = lax.broadcasted_iota(jnp.int32, core.shape, 1)
     a_ref[...] = core
     t_ref[...] = (rows == cols).astype(f32)
-
-
-def run_inverse(a_ref, t_ref, start, stop):
+    panel_ref[0], panel_ref[1] = a_ref[:8, :], t_ref[:8, :]
+    left_ref[...] = jnp.zeros_like(left_ref)
+    right_ref[...] = jnp.zeros_like(right_ref)
+
+
+def run_inverse(state, start, stop):
+    a_ref, t_ref, panel_ref, left_ref, right_ref = state
     size = a_ref.shape[0]
     rows = lax.broadcasted_iota(jnp.int32, (size, size), 0)
 
     def step(b, carry):
         first = pl.multiple_of(b * 8, 8)
-        line, made = a_ref[pl.ds(first, 8), :], t_ref[pl.ds(first, 8), :]
-        factors = panel_factor(pltpu.roll(line, lax.rem(size - first, size), 1))
-        line = functools.reduce(jnp.add, [f * spread(line[i : i + 1, :], 8) for i, f in enumerate(factors)])
-        made = functools.reduce(jnp.add, [f * spread(made[i : i + 1, :], 8) for i, f in enumerate(factors)])
+        after = pl.multiple_of(lax.rem(first + 8, size), 8)
+        turn = lax.rem(size - first, size)
+        line, made = panel_ref[0], panel_ref[1]
+        change = mm(left_ref[...], right_ref[...], TN)
+        a_ref[...] = a_ref[...] - change[:, :size]
+        t_ref[...] = t_ref[...] - jnp.where(rows >= first, change[:, size:], 0.0)
+        factors, inverse = panel_factor(pltpu.roll(line, turn, 1))
+        line, made = weighed(factors, line), weighed(factors, made)
+        later, built = a_ref[pl.ds(after, 8), :], t_ref[pl.ds(after, 8), :]
         t_ref[pl.ds(first, 8), :] = made
+        block = pltpu.roll(later, turn, 1)
+        columns = [spread(block[:, i : i + 1], 8) for i in range(8)]
+        scales = [functools.reduce(jnp.add, [inverse[i, j] * columns[j] for j in range(i + 1)]) for i in range(8)]
+        panel_ref[0] = later - weighed(scales, line)
+        panel_ref[1] = built - weighed(scales, made)
         high, middle, low = thirds(jnp.concatenate([line, made], axis=1))
-        right = jnp.concatenate([high, middle, high, middle, low, high], axis=0)
-        left = jnp.concatenate([high, high, middle, middle, high, low], axis=0)[:, :size]
-        change = mm(left.astype(bf16), right.astype(bf16), TN)
-        a_ref[...] = a_ref[...] - change[:, :size]
-        t_ref[...] = t_ref[...] - jnp.where(rows >= first + 8, change[:, size:], 0.0)
+        right_ref[...] = jnp.concatenate([high, middle, high, middle, low, high], axis=0).astype(bf16)
+        left_ref[...] = jnp.concatenate([high, high, middle, middle, high, low], axis=0)[:, :size].astype(bf16)
         return carry
 
     lax.fori_loop(start, stop, step, 0)
@@ -305,7 +321,9 @@
     greet(place)
     rest = list(rest)
     sum_a, sum_b, rest = rest[:7], rest[7:14], rest[14:]
-    q_ref, p_ref, core_ref, a_ref, t_ref, c_ref, *rest = rest
+    q_ref, p_ref, core_ref, c_ref, *rest = rest
+    state, rest = rest[:5], rest[5:]
+    t_ref = state[1]
     load_rows(place, pivots, turned, points, factor, sum_a[0], loads)
     greeted()
     device_sum(place, *sum_a)
@@ -321,28 +339,27 @@
         for h in range(2):
             for j in range(6):
                 sum_b[0][k, :, 2 * j + h, :] = m_ref[pl.ds(128 * k + CHIPS * h, CHIPS), pl.ds(128 * j, 128)]
-    size = a_ref.shape[0]
+    size = t_ref.shape[0]
 
     def during_swap():
         pivot_terms(q_ref, p_ref, core_ref)
-        begin_inverse(shifted(core_ref[0, :size, :size], core_ref[1, :size, :size]), a_ref, t_ref)
+        begin_inverse(shifted(core_ref[0, :size, :size], core_ref[1, :size, :size]), state)
 
     def during_scatter():
-        run_inverse(a_ref, t_ref, 0, 12)
+        run_inverse(state, 0, 16)
 
     def during_gather():
-        run_inverse(a_ref, t_ref, 12, 16)
         turned = t_ref[...].T
         w_ref[:size, :size] = turned
         w_ref[size:, :size] = jnp.zeros((size, size), f32)
         c10 = exact(core_ref[0, size:, :size] - core_ref[1, size:, :size], turned)
         c_ref[...] = c10
         g1 = core_ref[1, size:, size:] + exact(c10, c10, NT)
-        begin_inverse(shifted(core_ref[0, size:, size:], g1), a_ref, t_ref)
-        run_inverse(a_ref, t_ref, 0, 8)
+        begin_inverse(shifted(core_ref[0, size:, size:], g1), state)
+        run_inverse(state, 0, 12)
 
     def on_the_way_back():
-        run_inverse(a_ref, t_ref, 8, 16)
+        run_inverse(state, 12, 16)
         t1 = t_ref[...]
         w_ref[size:, size:] = t1.T
         w_ref[:size, size:] = -exact(w_ref[:size, :size], exact(t1, c_ref[...]), NT)
@@ -381,6 +398,9 @@
             pltpu.VMEM((half, 2 * width), f32),
             pltpu.VMEM((2, size, size), f32),
             *[pltpu.VMEM((half, half), f32)] * 3,
+            pltpu.VMEM((2, 8, half), f32),
+            pltpu.VMEM((48, half), bf16),
+            pltpu.VMEM((48, 2 * half), bf16),
             pltpu.VMEM((wide, size), bf16),
             pltpu.VMEM((wide, size), bf16),
             pltpu.VMEM((4 * width, size), bf16),

time: 70.1 us -> 68.3 us (0.974)
  Pallas kernels: 67.4 us -> 65.6 us
    pallas_call x1, Pallas kernels: 61.8 us -> 60 us  [main(): pl.pallas_call(main_kernel, out_shape=(jax.ShapeDtypeStruct((count, size)...]
where the time goes in v5:
time: 68.3 us; the launch traced here: 68.2 us
  Pallas kernels  65.6 us (96%)
  local copies, waits for them, and re-layouts  1.9 us (3%)
    pallas_call x1, Pallas kernels, main(): pl.pallas_call(main_kernel, out_shape=(jax.ShapeDtypeStruct((count, size)...  60 us
    pallas_call x1, Pallas kernels, columns(): pl.pallas_call(functools.partial(columns_kernel, scale=1.0 / count), out_...  5.61 us
    unnamed x4, local copies, waits for them, and re-layouts  1.9 us

profile of v5, /device:TPU:1, one launch (start us, length us, event | category | flops | bytes accessed | tf_op | source)
XLA Modules:
  0.0 68.2 jit_solution(15443084380207947380)
XLA Ops:
  0.6 0.0 copy-start
  0.6 1.2 %copy-done = f32[4096,64]{0,1:T(8,128)S(1)} copy-done((f32[4096,64]{0,1:T(8,128)S(1)}, f32[4096,64]{0,1:T(8,128)}, u32[]{:S(2)}) %copy-start) | copy-done | bytes 1048600
  1.9 0.0 copy-start.1
  1.9 0.7 copy-done.1
  2.5 60.0 %shard_map.50 = (f32[4096,256]{1,0:T(8,128)S(1)}, f32[256,768]{1,0:T(8,128)S(1)}, f32[256,256]{1,0:T(8,128)S(1)}) custom-call(s32[2,128]{1,0:T(2,128)S(1)} %copy-done.1, f32[64,4096]{1,0:T(8,128)S(1)} %bitcast.1, f32[4096,512]{1,0:T(8,128)} %factor_hbm.1), custom_call_target="tpu_custom_call" | custom-call | tf_op jit(solution)/shard_map/pallas_call | solution.py:380
  62.6 5.6 %shard_map.51 = (f32[4096,256]{1,0:T(8,128)}, f32[256,768]{1,0:T(8,128)}) custom-call(f32[4096,256]{1,0:T(8,128)S(1)} %get-tuple-element.5.r_ref, f32[256,256]{1,0:T(8,128)S(1)} %get-tuple-element.6.w_ref, f32[256,768]{1,0:T(8,128)S(1)} %get-tuple-element.7.m_ref), custom_call_target="tpu_custom_call" | custom-call | tf_op jit(solution)/shard_map/pallas_call | solution.py:438
Async XLA Ops:
  0.6 1.2 %copy-start = (f32[4096,64]{0,1:T(8,128)S(1)}, f32[4096,64]{0,1:T(8,128)}, u32[]{:S(2)}) copy-start(f32[4096,64]{0,1:T(8,128)} %param.3) | copy-start | bytes 3145732
  1.9 0.7 copy-start.1

commit v6 on v5

--- a/solution.py
+++ b/solution.py
@@ -356,10 +356,10 @@
         c_ref[...] = c10
         g1 = core_ref[1, size:, size:] + exact(c10, c10, NT)
         begin_inverse(shifted(core_ref[0, size:, size:], g1), state)
-        run_inverse(state, 0, 12)
+        run_inverse(state, 0, 14)
 
     def on_the_way_back():
-        run_inverse(state, 12, 16)
+        run_inverse(state, 14, 16)
         t1 = t_ref[...]
         w_ref[size:, size:] = t1.T
         w_ref[:size, size:] = -exact(w_ref[:size, :size], exact(t1, c_ref[...]), NT)
@@ -433,7 +433,7 @@
         g_ref[:, wide:] = exact(turned, exact(m_ref[:, wide:], w)) * scale
 
 
-def columns(r, w, m, tile=1024):
+def columns(r, w, m, tile=2048):
     count, size = r.shape
     return pl.pallas_call(
         functools.partial(columns_kernel, scale=1.0 / count),

time: 68.3 us -> 67.9 us (level)
  no operation moved by 1% of the time
where the time goes in v6:
time: 67.9 us; the launch traced here: 67.8 us
  Pallas kernels  65.2 us (96%)
  local copies, waits for them, and re-layouts  1.9 us (3%)
    pallas_call x1, Pallas kernels, main(): pl.pallas_call(main_kernel, out_shape=(jax.ShapeDtypeStruct((count, size)...  60 us
    pallas_call x1, Pallas kernels, columns(): pl.pallas_call(functools.partial(columns_kernel, scale=1.0 / count), out_...  5.22 us
    unnamed x4, local copies, waits for them, and re-layouts  1.9 us

profile of v6, /device:TPU:1, one launch (start us, length us, event | category | flops | bytes accessed | tf_op | source)
XLA Modules:
  0.0 67.8 jit_solution(5761755700182069453)
XLA Ops:
  0.6 0.0 copy-start
  0.6 1.2 %copy-done = f32[4096,64]{0,1:T(8,128)S(1)} copy-done((f32[4096,64]{0,1:T(8,128)S(1)}, f32[4096,64]{0,1:T(8,128)}, u32[]{:S(2)}) %copy-start) | copy-done | bytes 1048600
  1.9 0.0 copy-start.1
  1.9 0.7 copy-done.1
  2.5 60.0 %shard_map.50 = (f32[4096,256]{1,0:T(8,128)S(1)}, f32[256,768]{1,0:T(8,128)S(1)}, f32[256,256]{1,0:T(8,128)S(1)}) custom-call(s32[2,128]{1,0:T(2,128)S(1)} %copy-done.1, f32[64,4096]{1,0:T(8,128)S(1)} %bitcast.1, f32[4096,512]{1,0:T(8,128)} %factor_hbm.1), custom_call_target="tpu_custom_call" | custom-call | tf_op jit(solution)/shard_map/pallas_call | solution.py:380
  62.6 5.2 %shard_map.51 = (f32[4096,256]{1,0:T(8,128)}, f32[256,768]{1,0:T(8,128)}) custom-call(f32[4096,256]{1,0:T(8,128)S(1)} %get-tuple-element.5.r_ref, f32[256,256]{1,0:T(8,128)S(1)} %get-tuple-element.6.w_ref, f32[256,768]{1,0:T(8,128)S(1)} %get-tuple-element.7.m_ref), custom_call_target="tpu_custom_call" | custom-call | tf_op jit(solution)/shard_map/pallas_call | solution.py:438
Async XLA Ops:
  0.6 1.2 %copy-start = (f32[4096,64]{0,1:T(8,128)S(1)}, f32[4096,64]{0,1:T(8,128)}, u32[]{:S(2)}) copy-start(f32[4096,64]{0,1:T(8,128)} %param.3) | copy-start | bytes 3145732
  1.9 0.7 %copy-start.1 = (s32[2,128]{1,0:T(2,128)S(1)}, s32[2,128]{1,0:T(2,128)}, u32[]{:S(2)}) copy-start(s32[2,128]{1,0:T(2,128)} %pivots_hbm.1) | copy-start | bytes 3076
